TPU v7x, 128 devices: a whole 4x4x4 slice. The times are simulated.
128 devices in a mesh: row: 8 (over z, core), col: 16 (over x, y).
Axes of the slice: x: 4, y: 4, z: 4, core: 2. Of those that a mesh axis runs over, the one named last changes fastest.
Arguments:
- far_field: float32 [16384, 16384], P('row', 'col'), may hold values from -4 to 4, as said below
- inverses: float32 [2, 256, 256], replicated, may hold values from -0.05 to 0.06, as said below
- test_table: float32 [524288, 128], P(('row', 'col')), may hold values from -1.5 to 1.5
- trial_table: float32 [524288, 128], P(('row', 'col')), may hold values from -1.5 to 1.5
- tile_list: int32 [2048, 2], P(('row', 'col')), may hold values from 0 to 127, as said below
- tile_nodes: int32 [2048, 256], P(('row', 'col')), may hold values from 0 to 4095
- strokes: float32 [16384, 256], P('col'), may hold values from -0.046875 to 0.046875
Outputs:
- factored: float32 [16384, 16384], P('row', 'col')
- stroke_image: float32 [16384, 256], P('row')
Inputs may be any that keep to these rules, and one draw needn't show every extreme that they name: `tile_list`: tile t lies in the block rows held by the grid row of its pair owner (owners in row-major order of the device grid). At most 2 tiles of one owner fall in the block columns of one grid column, and in every grid row some grid column receives exactly 2 tiles from every owner of that row. Duplicate blocks may occur. `tile_nodes`: node indices refer to the owner's own 4096 table rows. `far_field`: entries of order one with a dominant diagonal between 2 and 4. `inverses`: each inverse has a positive diagonal and full off-diagonal entries.
All inputs are finite; a program needn't handle non-finite values.
Results may differ from a plain program's by a relative error of at most 0.0001.
Values sent between devices are 32-bit elements; how exact they have to be, the bound alone decides.
A program may use at most 128 MiB of HBM per device.

v0:
```python
import jax
import jax.numpy as jnp
from jax import lax
from jax.sharding import PartitionSpec as P


def broadcast(value, axis, source):
    kept = jnp.where(lax.axis_index(axis) == source, value, 0).astype(value.dtype)
    return lax.psum(kept, axis)


def rows_share(block):
    return broadcast(block, "row", 0)


def on_device(far_field, inverses, test_table, trial_table, tile_list, tile_nodes, strokes):
    highest = lax.Precision.HIGHEST
    col_count = lax.axis_size("col")
    row_index = lax.axis_index("row")
    col_index = lax.axis_index("col")
    rows_local, cols_local = far_field.shape
    tile = test_table.shape[1]
    width = inverses.shape[1]
    owned = tile_list.shape[0]
    capacity = 2 * ((owned + col_count - 1) // col_count)
    block_rows = rows_local // tile
    block_cols = cols_local // tile
    left = test_table[tile_nodes]
    right = trial_table[tile_nodes]
    pieces = jnp.einsum(
        "tqi,tqj->tij", left, right, precision=highest, preferred_element_type=jnp.float32
    )
    pieces = pieces.reshape(owned, tile * tile)
    target = tile_list[:, 1] // block_cols
    position = jnp.arange(owned, dtype=jnp.int32)
    earlier = (target[None, :] == target[:, None]) & (position[None, :] < position[:, None])
    slot = target * capacity + jnp.sum(earlier.astype(jnp.int32), axis=1)
    picked = jnp.arange(col_count * capacity, dtype=jnp.int32)[:, None] == slot[None, :]
    local_block = (tile_list[:, 0] - row_index * block_rows) * block_cols + tile_list[
        :, 1
    ] % block_cols
    outgoing = jnp.dot(
        picked.astype(jnp.float32), pieces, precision=highest, preferred_element_type=jnp.float32
    )
    outgoing = outgoing.reshape(col_count, capacity, tile * tile)
    labels = jnp.sum(jnp.where(picked, local_block[None, :] + 1, 0), axis=1) - 1
    labels = labels.reshape(col_count, capacity)
    arrived, spots = (
        lax.all_to_all(outgoing, "col", split_axis=0, concat_axis=0, tiled=True),
        lax.all_to_all(labels, "col", split_axis=0, concat_axis=0, tiled=True),
    )
    arrived = arrived.reshape(col_count * capacity, tile * tile)
    spots = spots.reshape(col_count * capacity)
    placing = (
        jnp.arange(block_rows * block_cols, dtype=jnp.int32)[:, None] == spots[None, :]
    ).astype(jnp.float32)
    near = jnp.dot(placing, arrived, precision=highest, preferred_element_type=jnp.float32)
    near = (
        near.reshape(block_rows, block_cols, tile, tile)
        .transpose(0, 2, 1, 3)
        .reshape(rows_local, cols_local)
    )
    matrix = far_field + near
    global_rows = row_index * rows_local + jnp.arange(rows_local, dtype=jnp.int32)
    global_cols = col_index * cols_local + jnp.arange(cols_local, dtype=jnp.int32)
    first_grid_col = col_index == 0
    for panel in range(2):
        low = panel * width
        high = low + width
        lower = jnp.dot(
            matrix[:, low:high],
            inverses[panel],
            precision=highest,
            preferred_element_type=jnp.float32,
        )
        lower = jnp.where(global_rows[:, None] >= high, lower, 0.0)
        lower_all = broadcast(lower, "col", 0)
        upper = jnp.where(global_cols[None, :] >= high, matrix[low:high, :], 0.0)
        upper_all = rows_share(upper)
        matrix = matrix - jnp.dot(
            lower_all, upper_all, precision=highest, preferred_element_type=jnp.float32
        )
        renewed = jnp.where(global_rows[:, None] >= high, lower_all, matrix[:, low:high])
        matrix = matrix.at[:, low:high].set(jnp.where(first_grid_col, renewed, matrix[:, low:high]))
    partial_image = jnp.dot(matrix, strokes, precision=highest, preferred_element_type=jnp.float32)
    image = lax.psum(partial_image, "col")
    return (matrix, image)


def solution(mesh):
    return jax.shard_map(
        on_device,
        mesh=mesh,
        in_specs=(
            P("row", "col"),
            P(),
            P(("row", "col"), None),
            P(("row", "col"), None),
            P(("row", "col"), None),
            P(("row", "col"), None),
            P("col", None),
        ),
        out_specs=(P("row", "col"), P("row", None)),
        check_vma=False,
    )
```

profile of v0, /device:TPU:72, one launch (start us, length us, event | category | flops | bytes accessed | tf_op | source)
XLA Modules:
  0.0 571.8 jit_solution(1673368568827543794)
XLA Ops:
  7.2 0.8 fusion.29
  8.0 0.8 fusion.30
  9.8 7.4 %all-to-all-start = ((s32[16,1,2]{2,1,0:T(1,128)}), s32[16,1,2]{2,1,0:T(1,128)S(1)}, u32[]{:S(2)}, u32[]{:S(2)}) async-start(s32[16,1,2]{2,1,0:T(1,128)} %bitcast.3), calls=%async_computation | async-start | bytes 16384 | tf_op jit(solution)/shard_map/all_to_all | solution.py:50
  17.2 0.7 fusion.18
  17.9 14.2 %gather_fusion = f32[4096,128]{1,0:T(8,128)} fusion(f32[4096,128]{1,0:T(8,128)S(1)} %copy-done, s32[4096]{0:T(1024)S(1)} %broadcast_clamp_fusion), kind=kCustom, calls=%fused_computation | custom fusion | bytes 4210688 | tf_op jit(solution)/shard_map/gather | solution.py:28
  32.1 15.9 %gather_fusion.1 = f32[4096,128]{1,0:T(8,128)} fusion(f32[4096,128]{1,0:T(8,128)} %param.14, s32[4096]{0:T(1024)S(1)} %broadcast_clamp_fusion), kind=kCustom, calls=%fused_computation.1 | custom fusion | bytes 4210688 | tf_op jit(solution)/shard_map/gather | solution.py:29
  48.1 5.1 fusion.31
  53.1 1.2 reshape.237
  54.3 2.2 fusion.19
  56.6 2.9 copy.19
  59.5 7.2 %all-to-all-start.1 = ((f32[16,2,16384]{2,1,0:T(2,128)}), f32[16,2,16384]{2,1,0:T(2,128)S(1)}, u32[]{:S(2)}, u32[]{:S(2)}) async-start(f32[16,2,16384]{2,1,0:T(2,128)} %copy.19), calls=%async_computation.1 | async-start | bytes 4194304 | tf_op jit(solution)/shard_map/all_to_all | solution.py:49
  68.3 26.4 %all-to-all-done.1 = f32[16,2,16384]{2,1,0:T(2,128)S(1)} async-done(((f32[16,2,16384]{2,1,0:T(2,128)}), f32[16,2,16384]{2,1,0:T(2,128)S(1)}, u32[]{:S(2)}, u32[]{:S(2)}) %all-to-all-start.1) | async-done | bytes 2097184 | tf_op jit(solution)/shard_map/all_to_all | solution.py:49
  94.7 2.4 reshape.215
  97.1 7.3 %fusion.4 = f32[16,8,128,128]{3,1,2,0:T(8,128)} fusion(s32[32]{0:T(128)S(1)} %eq.93, s32[16,8]{1,0:T(8,128)S(1)} %multiply_add_fusion, f32[32,16384]{1,0:T(8,128)} %reshape.215), kind=kOutput, calls=%fused_computation.14 | convolution fusion | flops 805310464 | bytes 10486400 | tf_op jit(solution)/shard_map/dot_general | solution.py:57
  104.4 12.1 %bitcast_add_fusion = f32[2048,1024]{1,0:T(8,128)} fusion(f32[2048,1024]{1,0:T(8,128)} %param.11, f32[256,8,8,128]{3,2,1,0:T(8,128)} %bitcast.63), kind=kLoop, calls=%fused_computation.2 | loop fusion | flops 2097152 | bytes 25165824 | tf_op jit(solution)/shard_map/add | solution.py:63
  116.6 2.4 fusion.9
  119.1 4.7 fusion.1
  124.8 52.6 %all-reduce.8.cloned.1.call-done = f32[256,1024]{1,0:T(8,128)} async-done(((f32[256,1024]{1,0:T(8,128)}), f32[256,1024]{1,0:T(8,128)}) %all-reduce.8.cloned.1.call-update) | async-done | bytes 1048592 | tf_op jit(solution)/shard_map/psum | solution.py:9
  177.4 97.8 %all-reduce.6.cloned.1.call-done = f32[2048,256]{1,0:T(8,128)} async-done(((f32[2048,256]{1,0:T(8,128)}), f32[2048,256]{1,0:T(8,128)}) %all-reduce.6.cloned.1.call-update) | async-done | bytes 2097168 | tf_op jit(solution)/shard_map/psum | solution.py:9
  275.2 10.6 %convolution_subtract_fusion.1 = f32[2048,1024]{1,0:T(8,128)S(1)} fusion(f32[2048,1024]{1,0:T(8,128)} %bitcast_add_fusion, f32[2048,256]{1,0:T(8,128)} %all-reduce.6.cloned.1.call-done, f32[256,1024]{1,0:T(8,128)} %all-reduce.8.cloned.1.call-done), kind=kOutput, calls=%fused_computation.4 | convolution fusion | flops 6444548096 | bytes 19922944 | tf_op jit(solution)/shard_map/dot_general | solution.py:80
  285.8 1.2 fusion.2
  287.1 3.4 copy-done.3
  290.5 1.1 fusion.8
  291.7 4.7 fusion
  297.4 53.0 %all-reduce.12.cloned.1.call-done = f32[256,1024]{1,0:T(8,128)} async-done(((f32[256,1024]{1,0:T(8,128)}), f32[256,1024]{1,0:T(8,128)}) %all-reduce.12.cloned.1.call-update) | async-done | bytes 1048592 | tf_op jit(solution)/shard_map/psum | solution.py:9
  350.4 97.7 %all-reduce.10.cloned.1.call-done = f32[2048,256]{1,0:T(8,128)} async-done(((f32[2048,256]{1,0:T(8,128)}), f32[2048,256]{1,0:T(8,128)}) %all-reduce.10.cloned.1.call-update) | async-done | bytes 2097168 | tf_op jit(solution)/shard_map/psum | solution.py:9
  448.1 10.6 %convolution_subtract_fusion = f32[2048,1024]{1,0:T(8,128)S(1)} fusion(f32[2048,1024]{1,0:T(8,128)} %copy-done.3, f32[2048,256]{1,0:T(8,128)} %all-reduce.10.cloned.1.call-done, f32[256,1024]{1,0:T(8,128)} %all-reduce.12.cloned.1.call-done), kind=kOutput, calls=%fused_computation.3 | convolution fusion | flops 6444548096 | bytes 19922944 | tf_op jit(solution)/shard_map/dot_general | solution.py:80
  458.7 1.4 fusion.3
  460.0 3.4 copy-done.2
  463.4 8.3 %fusion.32 = f32[2048,256]{1,0:T(8,128)} fusion(f32[2048,1024]{1,0:T(8,128)S(1)} %fusion.3, f32[1024,256]{1,0:T(8,128)S(1)} %copy-done.7), kind=kOutput, calls=%fused_computation.69 | convolution fusion | flops 6442450944 | bytes 11534336 | tf_op jit(solution)/shard_map/dot_general | solution.py:85
  471.7 90.5 %all-reduce.14.cloned.1.call-done = f32[2048,256]{1,0:T(8,128)} async-done(((f32[2048,256]{1,0:T(8,128)}), f32[2048,256]{1,0:T(8,128)}) %all-reduce.14.cloned.1.call-update) | async-done | bytes 2097168 | tf_op jit(solution)/shard_map/psum | solution.py:86
  562.3 3.0 copy.38
  (45 shorter events, 4.6 us)
Async XLA Ops:
  7.2 10.8 %copy-start = (f32[4096,128]{1,0:T(8,128)S(1)}, f32[4096,128]{1,0:T(8,128)}, u32[]{:S(2)}) copy-start(f32[4096,128]{1,0:T(8,128)} %param.13) | copy-start | bytes 6291460
  9.8 49.7 %all-to-all-start = ((s32[16,1,2]{2,1,0:T(1,128)}), s32[16,1,2]{2,1,0:T(1,128)S(1)}, u32[]{:S(2)}, u32[]{:S(2)}) async-start(s32[16,1,2]{2,1,0:T(1,128)} %bitcast.3), calls=%async_computation | async-start | bytes 16384 | tf_op jit(solution)/shard_map/all_to_all | solution.py:50
  32.1 15.9 %copy-start.6 = (f32[4096,128]{1,0:T(8,128)S(1)}, f32[4096,128]{1,0:T(8,128)}, u32[]{:S(2)}) copy-start(f32[4096,128]{1,0:T(8,128)} %gather_fusion) | copy-start | bytes 6291460
  59.5 35.2 %all-to-all-start.1 = ((f32[16,2,16384]{2,1,0:T(2,128)}), f32[16,2,16384]{2,1,0:T(2,128)S(1)}, u32[]{:S(2)}, u32[]{:S(2)}) async-start(f32[16,2,16384]{2,1,0:T(2,128)} %copy.19), calls=%async_computation.1 | async-start | bytes 4194304 | tf_op jit(solution)/shard_map/all_to_all | solution.py:49
  66.7 110.7 %all-reduce.8.cloned.1.call-start = ((), (), s32[]{:S(2)}) async-start(), calls=%async_computation.3 | async-start | bytes 2097152 | tf_op jit(solution)/shard_map/psum | solution.py:9
  116.6 2.5 copy-start.8
  119.0 156.2 %all-reduce.6.cloned.1.call-start = ((), (), s32[]{:S(2)}) async-start(), calls=%async_computation.2 | async-start | bytes 4194304 | tf_op jit(solution)/shard_map/psum | solution.py:9
  123.8 226.6 %all-reduce.12.cloned.1.call-start = ((), (), s32[]{:S(2)}) async-start(), calls=%async_computation.5 | async-start | bytes 2097152 | tf_op jit(solution)/shard_map/psum | solution.py:9
  275.2 10.6 %copy-start.4 = (f32[2048,256]{1,0:T(8,128)S(1)}, f32[2048,256]{1,0:T(8,128)}, u32[]{:S(2)}) copy-start(f32[2048,256]{1,0:T(8,128)} %all-reduce.6.cloned.1.call-done) | copy-start | bytes 6291460
  287.1 3.4 copy-start.3
  291.6 156.4 %all-reduce.10.cloned.1.call-start = ((), (), s32[]{:S(2)}) async-start(), calls=%async_computation.4 | async-start | bytes 4194304 | tf_op jit(solution)/shard_map/psum | solution.py:9
  296.5 265.8 %all-reduce.14.cloned.1.call-start = ((), (), s32[]{:S(2)}) async-start(), calls=%async_computation.6 | async-start | bytes 4194304 | tf_op jit(solution)/shard_map/psum | solution.py:86
  448.0 10.6 %copy-start.5 = (f32[2048,256]{1,0:T(8,128)S(1)}, f32[2048,256]{1,0:T(8,128)}, u32[]{:S(2)}) copy-start(f32[2048,256]{1,0:T(8,128)} %all-reduce.10.cloned.1.call-done) | copy-start | bytes 6291460
  458.6 4.8 copy-start.7
  460.0 3.4 copy-start.2
  471.7 93.6 %copy-start.1 = (f32[4096,128]{1,0:T(8,128)S(1)}, f32[4096,128]{1,0:T(8,128)}, u32[]{:S(2)}) copy-start(f32[4096,128]{1,0:T(8,128)} %param.13) | copy-start | bytes 6291460
Sparse Core Ops, SparseCore 0:
  119.1 58.2 all-reduce.7
  181.3 93.8 all-reduce.5
  291.8 58.5 all-reduce.11
  354.1 93.8 all-reduce.9
  471.8 90.3 all-reduce.13
where the time goes:
time: 574 us; the launch traced here: 572 us
  waiting for transfers between devices  418 us (73%)
  matrix products  53.5 us (9%)
  local copies, waits for them, and re-layouts  47.8 us (8%)
  other arithmetic  23 us (4%)
  starting transfers between devices  15.5 us (3%)
  between operations  14 us (2%)
    psum x4, waiting for transfers between devices, broadcast(): return lax.psum(kept, axis)  301 us
    psum x1, waiting for transfers between devices, on_device(): image = lax.psum(partial_image, 'col')  90.5 us
    all_to_all x1, waiting for transfers between devices, on_device(): lax.all_to_all(outgoing, 'col', split_axis=0, concat_axis=0, tiled=True)  26.4 us
    dot_general x2, matrix products, on_device(): jnp.dot(lower_all, upper_all, precision=highest, preferred_element_type=j...  21.1 us
    gather x1, local copies, waits for them, and re-layouts, on_device(): right = trial_table[tile_nodes]  15.9 us
    gather x1, local copies, waits for them, and re-layouts, on_device(): left = test_table[tile_nodes]  14.2 us
    add x1, other arithmetic, on_device(): matrix = far_field + near  12.1 us
  transfers between devices with their start and end apart: 7, of which 6 were waited for; matrix products, arithmetic and copies ran while one was open for 10% of the time, Pallas kernels for 0%

commit v1 on v0

v1 whole, which is shorter than its diff:
```python
import functools

import jax
import jax.numpy as jnp
from jax import lax
from jax.experimental import pallas as pl
from jax.experimental.pallas import tpu as pltpu
from jax.sharding import PartitionSpec as P

MESH = pl.DeviceIdType.MESH
HIGH = lax.Precision.HIGH
F32 = jnp.float32
VMEM = pltpu.VMEM
DMA = pltpu.SemaphoreType.DMA

LINK_TREE = (
    (0, 1, 2, 3), (1, 1, 1, 4), (3, 1, 1, 3), (3, 4, 3, 3),
    (0, 0, 4, 0), (1, 1, 0, 1), (3, 1, 0, 3), (0, 3, 0, 0),
    (0, 0, 2, 2), (0, 0, 2, 1), (0, 1, 2, 3), (0, 3, 2, 2),
    (4, 2, 2, 2), (2, 2, 2, 1), (2, 1, 1, 3), (2, 3, 3, 3),
)
TREE_DEPTH = (
    (0, 3, 4, 3, 1, 2, 3, 2, 2, 3, 4, 3, 3, 4, 5, 4),
    (0, 1, 2, 3, 3, 2, 3, 4, 4, 3, 4, 5, 3, 2, 3, 4),
    (0, 3, 4, 3, 3, 4, 5, 4, 2, 3, 4, 3, 1, 2, 3, 2),
    (0, 3, 2, 1, 3, 4, 3, 2, 4, 5, 4, 3, 3, 4, 3, 2),
)
STEPS_X = (1, 0, 3, 0)
STEPS_Y = (0, 1, 0, 3)


def table(values, index):
    found = jnp.int32(0)
    for at, value in enumerate(values):
        if value:
            found = found + jnp.where(index == at, jnp.int32(value), jnp.int32(0))
    return found


def mod4(value):
    return lax.rem(value, 4)


def dot(a, b):
    return jnp.dot(a, b, precision=HIGH, preferred_element_type=F32)


def pieces_kernel(tiles_ref, nodes_ref, test_ref, trial_ref, out_ref, left, right, count, label):
    owned, quad = nodes_ref.shape
    dests = out_ref.shape[0]
    tile = test_ref.shape[1]
    block_cols = 8
    block_rows = 16

    def clear(at, carry):
        count[at] = 0
        label[2 * at] = -1
        label[2 * at + 1] = -1
        return carry

    lax.fori_loop(0, dests, clear, 0)

    def one_tile(t, carry):
        for q in range(quad):
            node = nodes_ref[t, q]
            left[pl.ds(q, 1), :] = test_ref[pl.ds(node, 1), :]
            right[pl.ds(q, 1), :] = trial_ref[pl.ds(node, 1), :]
        piece = lax.dot_general(
            left[...], right[...], (((0,), (0,)), ((), ())), precision=HIGH, preferred_element_type=F32
        )
        block_row = lax.rem(tiles_ref[t, 0], block_rows)
        block_col = tiles_ref[t, 1]
        dest = lax.div(block_col, block_cols)
        slot = count[dest]
        count[dest] = slot + 1
        label[2 * dest + slot] = block_row * block_cols + lax.rem(block_col, block_cols)
        out_ref[dest, pl.ds(pl.multiple_of(slot * tile, tile), tile), :] = piece
        return carry

    lax.fori_loop(0, owned, one_tile, 0)
    sublane = lax.broadcasted_iota(jnp.int32, (8, tile), 0)
    for d in range(dests):
        both = jnp.where(sublane == 0, label[2 * d], label[2 * d + 1])
        out_ref[d, 2 * tile : 2 * tile + 8, :] = both.astype(F32)


def make_pieces(tile_list, tile_nodes, test_table, trial_table, dests):
    tile = test_table.shape[1]
    quad = tile_nodes.shape[1]
    return pl.pallas_call(
        pieces_kernel,
        out_shape=jax.ShapeDtypeStruct((dests, 2 * tile + 8, tile), F32),
        in_specs=[
            pl.BlockSpec(memory_space=pltpu.SMEM),
            pl.BlockSpec(memory_space=pltpu.SMEM),
            pl.BlockSpec(memory_space=VMEM),
            pl.BlockSpec(memory_space=VMEM),
        ],
        out_specs=pl.BlockSpec(memory_space=VMEM),
        scratch_shapes=[
            VMEM((quad, tile), F32),
            VMEM((quad, tile), F32),
            pltpu.SMEM((dests,), jnp.int32),
            pltpu.SMEM((2 * dests,), jnp.int32),
        ],
        name="pieces",
    )(tile_list, tile_nodes, test_table, trial_table)


OFFSETS = sorted(
    ((dx, dy) for dx in range(4) for dy in range(4) if dx or dy),
    key=lambda o: -(min(o[0], 4 - o[0]) + min(o[1], 4 - o[1])),
)


def exchange_kernel(packed, arrived, send_sem, recv_sem, own_sem):
    row = lax.axis_index("row")
    col = lax.axis_index("col")
    x, y = lax.div(col, 4), lax.rem(col, 4)
    peers = [mod4(x + dx) * 4 + mod4(y + dy) for dx, dy in OFFSETS]
    barrier = pltpu.get_barrier_semaphore()
    for peer in peers:
        pl.semaphore_signal(barrier, inc=1, device_id=(row, peer), device_id_type=MESH)
    pl.semaphore_wait(barrier, len(peers))
    own = pltpu.make_async_copy(packed.at[col], arrived.at[col], own_sem)
    copies = []
    for k, peer in enumerate(peers):
        copies.append(
            pltpu.make_async_remote_copy(
                src_ref=packed.at[peer],
                dst_ref=arrived.at[col],
                send_sem=send_sem.at[k],
                recv_sem=recv_sem.at[k],
                device_id=(row, peer),
                device_id_type=MESH,
            )
        )
        copies[-1].start()
    own.start()
    own.wait()
    for copy in copies:
        copy.wait()


def exchange(packed):
    n = len(OFFSETS)
    return pl.pallas_call(
        exchange_kernel,
        out_shape=jax.ShapeDtypeStruct(packed.shape, F32),
        in_specs=[pl.BlockSpec(memory_space=VMEM)],
        out_specs=pl.BlockSpec(memory_space=pl.ANY),
        scratch_shapes=[DMA((n,)), DMA((n,)), DMA],
        compiler_params=pltpu.CompilerParams(collective_id=0, has_side_effects=True),
        name="exchange",
    )(packed)


def place_kernel(label_ref, far, arrived, out, block, tiles, in_sem, out_sem, tile_sem):
    rows, cols = block.shape
    chunks = 8
    size = rows // chunks
    tile = tiles.shape[2]
    bring = pltpu.make_async_copy(arrived, tiles, tile_sem)
    bring.start()

    def part(j):
        return pl.ds(j * size, size)

    ins = [pltpu.make_async_copy(far.at[part(j)], block.at[part(j)], in_sem.at[j]) for j in range(chunks)]
    outs = [pltpu.make_async_copy(block.at[part(j)], out.at[part(j)], out_sem.at[j]) for j in range(chunks)]
    for copy in ins:
        copy.start()
    bring.wait()
    for j in range(chunks):
        ins[j].wait()

        def add(s, carry):
            lab = label_ref[s]

            @pl.when((lab >= 0) & (lax.div(lab, 16) == j))
            def _():
                at = (
                    pl.ds(pl.multiple_of(lax.div(lab, 8) * tile, tile), tile),
                    pl.ds(pl.multiple_of(lax.rem(lab, 8) * tile, tile), tile),
                )
                piece = tiles[lax.div(s, 2), pl.ds(pl.multiple_of(lax.rem(s, 2) * tile, tile), tile), :]
                block[at] = block[at] + piece

            return carry

        lax.fori_loop(0, label_ref.shape[0], add, 0)
        outs[j].start()
    for copy in outs:
        copy.wait()


def place(labels, far, arrived):
    return pl.pallas_call(
        place_kernel,
        out_shape=jax.ShapeDtypeStruct(far.shape, F32),
        in_specs=[
            pl.BlockSpec(memory_space=pltpu.SMEM),
            pl.BlockSpec(memory_space=pl.ANY),
            pl.BlockSpec(memory_space=pl.ANY),
        ],
        out_specs=pl.BlockSpec(memory_space=pl.ANY),
        scratch_shapes=[VMEM(far.shape, F32), VMEM(arrived.shape, F32), DMA((8,)), DMA((8,)), DMA],
        name="place",
    )(labels, far, arrived)


P_CHUNKS = 32
P_ROWS = 64
Q_CHUNKS = 16
Q_ROWS = 32
C_CHUNKS = 8


def bcast_kernel(
    asm, p_ref, q_ref, c_ref, load_p, load_q, send_p, recv_p, send_q, recv_q, send_c, recv_c
):
    row = lax.axis_index("row")
    col = lax.axis_index("col")
    x, y = lax.div(col, 4), lax.rem(col, 4)
    z, core = lax.div(row, 2), lax.rem(row, 2)
    source = col == 0
    top = row == 0
    z_up = mod4(z + 1) * 2 + core
    z_down = mod4(z + 3) * 2 + core
    other = z * 2 + 1 - core
    neighbours = [mod4(x + STEPS_X[d]) * 4 + mod4(y + STEPS_Y[d]) for d in range(4)]
    link_tree = [table([LINK_TREE[v][d] for v in range(16)], col) for d in range(4)]
    depth = [table(TREE_DEPTH[t], col) for t in range(4)]

    barrier = pltpu.get_barrier_semaphore()
    for d in range(4):
        pl.semaphore_signal(barrier, inc=1, device_id=(row, neighbours[d]), device_id_type=MESH)
    for r in (z_up, z_down, other):
        pl.semaphore_signal(barrier, inc=1, device_id=(r, col), device_id_type=MESH)

    quarter = p_ref.shape[0] // 4

    def load_quarter(k):
        rows = pl.ds(pl.multiple_of(k * quarter, quarter), quarter)
        return pltpu.make_async_copy(asm.at[rows, pl.ds(0, 512)], p_ref.at[rows, :], load_p.at[k])

    load_rows = pltpu.make_async_copy(asm.at[pl.ds(0, 512), :], q_ref, load_q)

    @pl.when(source)
    def _():
        for k in range(4):
            load_quarter(k).start()

    @pl.when(top)
    def _():
        load_rows.start()

    pl.semaphore_wait(barrier, 7)

    @pl.when(top)
    def _():
        load_rows.wait()

    def p_copy(t, i, d):
        at = p_ref.at[
            pl.ds(pl.multiple_of(i * P_ROWS, P_ROWS), P_ROWS), pl.ds(t * 128, 128)
        ]
        return pltpu.make_async_remote_copy(
            src_ref=at,
            dst_ref=at,
            send_sem=send_p.at[d, i],
            recv_sem=recv_p.at[t, i],
            device_id=(row, neighbours[d]),
            device_id_type=MESH,
        )

    def q_copy(h, j, way, r):
        at = q_ref.at[pl.ds(pl.multiple_of(j * Q_ROWS, Q_ROWS), Q_ROWS), pl.ds(h * 512, 512)]
        return pltpu.make_async_remote_copy(
            src_ref=at,
            dst_ref=at,
            send_sem=send_q.at[h, j, way],
            recv_sem=recv_q.at[h, j],
            device_id=(r, col),
            device_id_type=MESH,
        )

    def c_copy(i, way, r, first):
        rows = pl.ds(pl.multiple_of(i * P_ROWS, P_ROWS), P_ROWS)
        here = c_ref.at[rows, :]
        start = pl.multiple_of(jnp.where(i < C_CHUNKS // 2, 256, 0), 256)
        return pltpu.make_async_remote_copy(
            src_ref=p_ref.at[rows, pl.ds(start, 256)] if first else here,
            dst_ref=here,
            send_sem=send_c.at[i, way],
            recv_sem=recv_c.at[i],
            device_id=(r, col),
            device_id_type=MESH,
        )

    lead = core == 0
    q_depth = [z + core, mod4(4 - z) + core]
    q_next = [(z_up, lead & (z < 3)), (z_down, lead & (z != 1))]
    c_depth = 6 + jnp.where(z == 2, 2, jnp.where(z == 0, 0, 1)) + core

    def step(s, carry):
        for t in range(4):
            i = s - depth[t]

            @pl.when((i >= 0) & (i < P_CHUNKS))
            def _(t=t, i=i):
                if t == 0:

                    @pl.when(source & (lax.rem(i, P_CHUNKS // 4) == 0))
                    def _():
                        load_quarter(lax.div(i, P_CHUNKS // 4)).wait()

                @pl.when(jnp.logical_not(source))
                def _():
                    p_copy(t, i, 0).wait_recv()

                for d in range(4):

                    @pl.when(link_tree[d] == t)
                    def _(d=d):
                        p_copy(t, i, d).start()

        for h in range(2):
            j = s - q_depth[h]

            @pl.when((j >= 0) & (j < Q_CHUNKS))
            def _(h=h, j=j):
                @pl.when(jnp.logical_not(top))
                def _():
                    q_copy(h, j, 0, other).wait_recv()

                @pl.when(lead)
                def _():
                    q_copy(h, j, 0, other).start()

                @pl.when(q_next[h][1])
                def _():
                    q_copy(h, j, 1, q_next[h][0]).start()

        i = s - c_depth

        @pl.when((i >= 0) & (i < C_CHUNKS))
        def _():
            @pl.when(top)
            def _():
                c_copy(i, 0, other, True).start()
                c_copy(i, 1, z_up, True).start()
                c_copy(i, 2, z_down, True).start()

            @pl.when(jnp.logical_not(top))
            def _():
                c_copy(i, 0, other, False).wait_recv()

                @pl.when(lead)
                def _():
                    c_copy(i, 0, other, False).start()

                @pl.when(lead & (z == 1))
                def _():
                    c_copy(i, 1, z_up, False).start()

        return carry

    lax.fori_loop(0, P_CHUNKS + 6, step, 0)

    @pl.when(top)
    def _():
        c_ref[0:256, :] = p_ref[0:256, 256:512]
        c_ref[256:512, :] = p_ref[256:512, 0:256]

    def drain_p(i, carry):
        for d in range(4):

            @pl.when(link_tree[d] < 4)
            def _(d=d):
                p_copy(0, i, d).wait_send()

        return carry

    lax.fori_loop(0, P_CHUNKS, drain_p, 0)

    def drain_q(j, carry):
        for h in range(2):

            @pl.when(lead)
            def _(h=h):
                q_copy(h, j, 0, other).wait_send()

            @pl.when(q_next[h][1])
            def _(h=h):
                q_copy(h, j, 1, q_next[h][0]).wait_send()

        return carry

    lax.fori_loop(0, Q_CHUNKS, drain_q, 0)

    def drain_c(i, carry):
        @pl.when(lead)
        def _():
            c_copy(i, 0, other, False).wait_send()

        @pl.when(top | (lead & (z == 1)))
        def _():
            c_copy(i, 1, z_up, False).wait_send()

        @pl.when(top)
        def _():
            c_copy(i, 2, z_down, False).wait_send()

        return carry

    lax.fori_loop(0, C_CHUNKS, drain_c, 0)


def bcast(asm):
    rows, cols = asm.shape
    vmem = pl.BlockSpec(memory_space=VMEM)
    return pl.pallas_call(
        bcast_kernel,
        out_shape=(
            jax.ShapeDtypeStruct((rows, 512), F32),
            jax.ShapeDtypeStruct((512, cols), F32),
            jax.ShapeDtypeStruct((512, 256), F32),
        ),
        in_specs=[pl.BlockSpec(memory_space=pl.ANY)],
        out_specs=(vmem, vmem, vmem),
        scratch_shapes=[
            DMA((4,)),
            DMA,
            DMA((4, P_CHUNKS)),
            DMA((4, P_CHUNKS)),
            DMA((2, Q_CHUNKS, 2)),
            DMA((2, Q_CHUNKS)),
            DMA((C_CHUNKS, 3)),
            DMA((C_CHUNKS,)),
        ],
        compiler_params=pltpu.CompilerParams(collective_id=1, has_side_effects=True),
        name="bcast",
    )(asm)


def update_kernel(asm_ref, p_ref, q_ref, c_ref, inv_ref, s_ref, out_ref, img_ref, u_ref):
    i = pl.program_id(0)
    row = lax.axis_index("row")
    first_col = lax.axis_index("col") == 0

    @pl.when(i == 0)
    def _():
        ratio = dot(c_ref[256:512, :], inv_ref[0])
        u_ref[0:256, :] = q_ref[0:256, :]
        u_ref[256:512, :] = q_ref[256:512, :] - dot(ratio, q_ref[0:256, :])

        @pl.when(first_col)
        def _():
            u_ref[0:256, 0:256] = jnp.zeros((256, 256), F32)
            u_ref[256:512, 0:512] = jnp.zeros((256, 512), F32)

    below0 = (row > 0) | (i > 0)
    below1 = (row > 0) | (i > 1)
    lower0 = jnp.where(below0, dot(p_ref[:, 0:256], inv_ref[0]), 0.0)
    rest = p_ref[:, 256:512] - dot(lower0, c_ref[0:256, :])
    lower1 = jnp.where(below1, dot(rest, inv_ref[1]), 0.0)
    out_ref[...] = asm_ref[...] - dot(jnp.concatenate([lower0, lower1], axis=1), u_ref[...])

    @pl.when(first_col)
    def _():
        out_ref[:, 0:256] = jnp.where(below0, lower0, asm_ref[:, 0:256])
        out_ref[:, 256:512] = jnp.where(below1, lower1, rest)

    img_ref[...] = dot(out_ref[...], s_ref[...])


def update(asm, p, q, c, inverses, strokes):
    rows, cols = asm.shape
    size = 256

    def whole(shape):
        return pl.BlockSpec(shape, lambda i: (0,) * len(shape))

    def tiles(width):
        return pl.BlockSpec((size, width), lambda i: (i, 0))

    return pl.pallas_call(
        update_kernel,
        grid=(rows // size,),
        out_shape=(
            jax.ShapeDtypeStruct((rows, cols), F32),
            jax.ShapeDtypeStruct((rows, strokes.shape[1]), F32),
        ),
        in_specs=[
            tiles(cols),
            tiles(512),
            whole(q.shape),
            whole(c.shape),
            whole(inverses.shape),
            whole(strokes.shape),
        ],
        out_specs=(tiles(cols), tiles(strokes.shape[1])),
        scratch_shapes=[VMEM((512, cols), F32)],
        name="update",
    )(asm, p, q, c, inverses, strokes)


def image_kernel(part, out, stage1, stage2, send_sem, recv_sem):
    row = lax.axis_index("row")
    col = lax.axis_index("col")
    x, y = lax.div(col, 4), lax.rem(col, 4)
    rows = part.shape[0]
    half = rows // 2
    big = half // 4
    small = big // 4
    across = [mod4(x + k) * 4 + y for k in range(4)]
    along = [x * 4 + mod4(y + k) for k in range(4)]

    barrier = pltpu.get_barrier_semaphore()
    for k in range(1, 4):
        pl.semaphore_signal(barrier, inc=1, device_id=(row, across[k]), device_id_type=MESH)
        pl.semaphore_signal(barrier, inc=1, device_id=(row, along[k]), device_id_type=MESH)
    pl.semaphore_wait(barrier, 6)

    outer = (x, y)
    inner = (y, x)
    outer_peers = (across, along)
    inner_peers = (along, across)

    def remote(src, dst, stage, h, k, peer):
        return pltpu.make_async_remote_copy(
            src_ref=src,
            dst_ref=dst,
            send_sem=send_sem.at[stage, h, k - 1],
            recv_sem=recv_sem.at[stage, h, k - 1],
            device_id=(row, peer),
            device_id_type=MESH,
        )

    def rows_at(start, count):
        return pl.ds(pl.multiple_of(start, count), count)

    order = (2, 1, 3)
    first, second, third, fourth = [], [], [], []
    for k in order:
        for h in range(2):
            to = mod4(outer[h] + k)
            copy = remote(
                part.at[rows_at(h * half + to * big, big), :], stage1.at[h, k - 1], 0, h, k, outer_peers[h][k]
            )
            copy.start()
            first.append((h, copy))
    for h in range(2):
        for g, copy in first:
            if g == h:
                copy.wait_recv()
        total = part[rows_at(h * half + outer[h] * big, big), :]
        for k in range(1, 4):
            total = total + stage1[h, k - 1]
        stage1[h, 3] = total
        for k in order:
            to = mod4(inner[h] + k)
            copy = remote(
                stage1.at[h, 3, rows_at(to * small, small), :], stage2.at[h, k - 1], 1, h, k, inner_peers[h][k]
            )
            copy.start()
            second.append((h, copy))
    for h in range(2):
        for g, copy in second:
            if g == h:
                copy.wait_recv()
        total = stage1[h, 3, rows_at(inner[h] * small, small), :]
        for k in range(1, 4):
            total = total + stage2[h, k - 1]
        mine = rows_at(h * half + outer[h] * big + inner[h] * small, small)
        out[mine, :] = total
        for k in order:
            copy = remote(out.at[mine, :], out.at[mine, :], 2, h, k, inner_peers[h][k])
            copy.start()
            third.append((h, copy))
    for h in range(2):
        for g, copy in third:
            if g == h:
                copy.wait_recv()
        mine = rows_at(h * half + outer[h] * big, big)
        for k in order:
            copy = remote(out.at[mine, :], out.at[mine, :], 3, h, k, outer_peers[h][k])
            copy.start()
            fourth.append((h, copy))
    for _, copy in fourth:
        copy.wait_recv()
    for _, copy in first + second + third + fourth:
        copy.wait_send()


def image_sum(part):
    rows, cols = part.shape
    vmem = pl.BlockSpec(memory_space=VMEM)
    return pl.pallas_call(
        image_kernel,
        out_shape=jax.ShapeDtypeStruct(part.shape, F32),
        in_specs=[vmem],
        out_specs=vmem,
        scratch_shapes=[
            VMEM((2, 4, rows // 8, cols), F32),
            VMEM((2, 3, rows // 32, cols), F32),
            DMA((4, 2, 3)),
            DMA((4, 2, 3)),
        ],
        compiler_params=pltpu.CompilerParams(collective_id=2, has_side_effects=True),
        name="image_sum",
    )(part)


def on_device(far_field, inverses, test_table, trial_table, tile_list, tile_nodes, strokes):
    packed = make_pieces(tile_list, tile_nodes, test_table, trial_table, 16)
    arrived = exchange(packed)
    labels = arrived[:, 256:258, 0].astype(jnp.int32).reshape(32)
    asm = place(labels, far_field, arrived)
    p, q, c = bcast(asm)
    factored, part = update(asm, p, q, c, inverses, strokes)
    image = image_sum(part)
    return factored, image


def solution(mesh):
    return jax.shard_map(
        on_device,
        mesh=mesh,
        in_specs=(
            P("row", "col"),
            P(),
            P(("row", "col"), None),
            P(("row", "col"), None),
            P(("row", "col"), None),
            P(("row", "col"), None),
            P("col", None),
        ),
        out_specs=(P("row", "col"), P("row", None)),
        check_vma=False,
    )
```

time: 574 us -> 249 us (0.43)
  waiting for transfers between devices: 418 us -> 0 us
  Pallas kernels: 0 us -> 240 us
  matrix products: 53.5 us -> 0 us
  local copies, waits for them, and re-layouts: 47.8 us -> 5.01 us
  other arithmetic: 23 us -> 1.18 us
  starting transfers between devices: 15.5 us -> 0 us
  between operations: 14 us -> 0.67 us
    psum x5 -> x0, waiting for transfers between devices: 392 us -> none  [the longest x4 301 us: broadcast(): return lax.psum(kept, axis)]
    pallas_call x0 -> x6, Pallas kernels: none -> 240 us  [the longest x1 114 us: bcast(): pl.pallas_call(bcast_kernel, out_shape=(jax.ShapeDtypeStruct((rows, 512),...]
    dot_general x8 -> x0, matrix products: 53.5 us -> none  [the longest x2 21.1 us: on_device(): jnp.dot(lower_all, upper_all, precision=highest, preferred_element_type=j...]
    gather x2 -> x0, local copies, waits for them, and re-layouts: 30.1 us -> none  [the longest x1 15.9 us: on_device(): right = trial_table[tile_nodes]]
    all_to_all x2 -> x0, waiting for transfers between devices: 26.4 us -> none  [the longest x1 26.4 us: on_device(): lax.all_to_all(outgoing, 'col', split_axis=0, concat_axis=0, tiled=True)]
    all_to_all x2 -> x0, starting transfers between devices: 14.6 us -> none  [the longest x1 7.39 us: on_device(): lax.all_to_all(labels, 'col', split_axis=0, concat_axis=0, tiled=True)]
    add x3 -> x0, other arithmetic: 12.9 us -> none  [the longest x1 12.1 us: on_device(): matrix = far_field + near]
  transfers between devices with their start and end apart: 7 -> 0, of which waited for: 6 -> 0; matrix products, arithmetic and copies ran while one was open for 10% -> 0% of each run, Pallas kernels for 0% -> 0%
where the time goes in v1:
time: 249 us; the launch traced here: 246 us
  Pallas kernels  240 us (96%)
  local copies, waits for them, and re-layouts  5.01 us (2%)
    pallas_call x1, Pallas kernels, bcast(): pl.pallas_call(bcast_kernel, out_shape=(jax.ShapeDtypeStruct((rows, 512),...  114 us
    pallas_call x1, Pallas kernels, image_sum(): pl.pallas_call(image_kernel, out_shape=jax.ShapeDtypeStruct(part.shape, F...  41.9 us
    pallas_call x1, Pallas kernels, exchange(): pl.pallas_call(exchange_kernel, out_shape=jax.ShapeDtypeStruct(packed.sha...  32.6 us
    pallas_call x1, Pallas kernels, update(): pl.pallas_call(update_kernel, grid=(rows // size,), out_shape=(jax.ShapeD...  26.5 us
    pallas_call x1, Pallas kernels, make_pieces(): pl.pallas_call(pieces_kernel, out_shape=jax.ShapeDtypeStruct((dests, 2 *...  14.6 us
    pallas_call x1, Pallas kernels, place(): pl.pallas_call(place_kernel, out_shape=jax.ShapeDtypeStruct(far.shape, F3...  10.1 us

profile of v1, /device:TPU:72, one launch (start us, length us, event | category | flops | bytes accessed | tf_op | source)
XLA Modules:
  0.0 246.4 jit_solution(8209518410258662753)
XLA Ops:
  0.6 1.4 copy.10.tiles_ref
  2.0 14.6 %pieces.1.packed = f32[16,264,128]{2,1,0:T(8,128)} custom-call(s32[16,2]{1,0:T(8,128)} %copy.10.tiles_ref, s32[16,256]{1,0:T(8,128)} %nodes_ref.1, f32[4096,128]{1,0:T(8,128)} %test_ref.1, f32[4096,128]{1,0:T(8,128)} %trial_ref.1), custom_call_target="tpu_custom_call" | custom-call | tf_op jit(solution)/shard_map/pieces/pallas_call | solution.py:90
  16.6 32.6 %exchange.1.arrived = f32[16,264,128]{2,1,0:T(8,128)} custom-call(f32[16,264,128]{2,1,0:T(8,128)} %pieces.1.packed), custom_call_target="tpu_custom_call" | custom-call | tf_op jit(solution)/shard_map/exchange/pallas_call | solution.py:147
  49.3 1.2 convert_reduce_fusion
  50.5 0.6 convert_element_type.8.label_ref
  51.1 10.1 %place.1.asm.asm_ref = f32[2048,1024]{1,0:T(8,128)} custom-call(s32[32]{0:T(128)} %convert_element_type.8.label_ref, f32[2048,1024]{1,0:T(8,128)} %far.1, f32[16,264,128]{2,1,0:T(8,128)} %exchange.1.arrived), custom_call_target="tpu_custom_call" | custom-call | tf_op jit(solution)/shard_map/place/pallas_call | solution.py:198
  61.1 113.7 %bcast.1 = (f32[2048,512]{1,0:T(8,128)}, f32[512,1024]{1,0:T(8,128)}, f32[512,256]{1,0:T(8,128)}) custom-call(f32[2048,1024]{1,0:T(8,128)} %place.1.asm.asm_ref), custom_call_target="tpu_custom_call" | custom-call | tf_op jit(solution)/shard_map/bcast/pallas_call | solution.py:423
  174.9 26.5 %update.1 = (f32[2048,1024]{1,0:T(8,128)}, f32[2048,256]{1,0:T(8,128)}) custom-call(f32[2048,1024]{1,0:T(8,128)} %place.1.asm.asm_ref, f32[2048,512]{1,0:T(8,128)} %get-tuple-element.7.p_ref, f32[512,1024]{1,0:T(8,128)} %get-tuple-element.8.q_ref, f32[512,256]{1,0:T(8,128)} %get-tuple-element.9.c_ref, f32[2,256,256]{2,1,0:T(8,128)} %inv_ref.1, f32[1024,256]{1,0:T(8,128)} %s_ref.1), custom_call_target="tpu_custom_call" | custom-call | tf_op jit(solution)/shard_map/update/pallas_call | solution.py:488
  201.4 41.9 %image_sum.1 = f32[2048,256]{1,0:T(8,128)} custom-call(f32[2048,256]{1,0:T(8,128)} %get-tuple-element.11.part), custom_call_target="tpu_custom_call" | custom-call | tf_op jit(solution)/shard_map/image_sum/pallas_call | solution.py:600
  243.3 3.0 %copy.12 = f32[2048,256]{1,0:T(8,128)} copy(f32[2048,256]{1,0:T(8,128)} %image_sum.1) | data formatting | bytes 4194304

commit v2 on v1

--- a/solution.py
+++ b/solution.py
@@ -1,5 +1,3 @@
-import functools
-
 import jax
 import jax.numpy as jnp
 from jax import lax
@@ -8,7 +6,6 @@
 from jax.sharding import PartitionSpec as P
 
 MESH = pl.DeviceIdType.MESH
-HIGH = lax.Precision.HIGH
 F32 = jnp.float32
 VMEM = pltpu.VMEM
 DMA = pltpu.SemaphoreType.DMA
@@ -41,8 +38,20 @@
     return lax.rem(value, 4)
 
 
+def split(a):
+    high = a.astype(jnp.bfloat16)
+    return high, (a - high.astype(F32)).astype(jnp.bfloat16)
+
+
+def dot_split(a, b):
+    def one(u, v):
+        return jnp.dot(u, v, preferred_element_type=F32)
+
+    return one(a[0], b[0]) + (one(a[0], b[1]) + one(a[1], b[0]))
+
+
 def dot(a, b):
-    return jnp.dot(a, b, precision=HIGH, preferred_element_type=F32)
+    return dot_split(split(a), split(b))
 
 
 def pieces_kernel(tiles_ref, nodes_ref, test_ref, trial_ref, out_ref, left, right, count, label):
@@ -65,9 +74,7 @@
             node = nodes_ref[t, q]
             left[pl.ds(q, 1), :] = test_ref[pl.ds(node, 1), :]
             right[pl.ds(q, 1), :] = trial_ref[pl.ds(node, 1), :]
-        piece = lax.dot_general(
-            left[...], right[...], (((0,), (0,)), ((), ())), precision=HIGH, preferred_element_type=F32
-        )
+        piece = dot(left[...].T, right[...])
         block_row = lax.rem(tiles_ref[t, 0], block_rows)
         block_col = tiles_ref[t, 1]
         dest = lax.div(block_col, block_cols)
@@ -155,7 +162,7 @@
     )(packed)
 
 
-def place_kernel(label_ref, far, arrived, out, block, tiles, in_sem, out_sem, tile_sem):
+def place_kernel(label_ref, far, arrived, s_ref, out, g_ref, block, tiles, in_sem, out_sem, tile_sem):
     rows, cols = block.shape
     chunks = 8
     size = rows // chunks
@@ -170,6 +177,7 @@
     outs = [pltpu.make_async_copy(block.at[part(j)], out.at[part(j)], out_sem.at[j]) for j in range(chunks)]
     for copy in ins:
         copy.start()
+    strokes = split(s_ref[...])
     bring.wait()
     for j in range(chunks):
         ins[j].wait()
@@ -190,23 +198,29 @@
 
         lax.fori_loop(0, label_ref.shape[0], add, 0)
         outs[j].start()
+        g_ref[part(j), :] = dot_split(split(block[part(j), :]), strokes)
     for copy in outs:
         copy.wait()
 
 
-def place(labels, far, arrived):
+def place(labels, far, arrived, strokes):
+    rows = far.shape[0]
     return pl.pallas_call(
         place_kernel,
-        out_shape=jax.ShapeDtypeStruct(far.shape, F32),
+        out_shape=(
+            jax.ShapeDtypeStruct(far.shape, F32),
+            jax.ShapeDtypeStruct((rows, strokes.shape[1]), F32),
+        ),
         in_specs=[
             pl.BlockSpec(memory_space=pltpu.SMEM),
             pl.BlockSpec(memory_space=pl.ANY),
             pl.BlockSpec(memory_space=pl.ANY),
+            pl.BlockSpec(memory_space=VMEM),
         ],
-        out_specs=pl.BlockSpec(memory_space=pl.ANY),
+        out_specs=(pl.BlockSpec(memory_space=pl.ANY), pl.BlockSpec(memory_space=VMEM)),
         scratch_shapes=[VMEM(far.shape, F32), VMEM(arrived.shape, F32), DMA((8,)), DMA((8,)), DMA],
         name="place",
-    )(labels, far, arrived)
+    )(labels, far, arrived, strokes)
 
 
 P_CHUNKS = 32
@@ -214,10 +228,13 @@
 Q_CHUNKS = 16
 Q_ROWS = 32
 C_CHUNKS = 8
-
-
-def bcast_kernel(
-    asm, p_ref, q_ref, c_ref, load_p, load_q, send_p, recv_p, send_q, recv_q, send_c, recv_c
+LAG = 8
+
+
+def panel_kernel(
+    asm, g_ref, inv_ref, s_ref, l_out, u_out, img, p_ref, q_ref, c_ref, l_ref, u_ref, us_ref, part,
+    stage1, stage2, load_p, load_q, send_p, recv_p, send_q, recv_q, send_c, recv_c, out_l, out_u,
+    send_i, recv_i
 ):
     row = lax.axis_index("row")
     col = lax.axis_index("col")
@@ -232,9 +249,12 @@
     link_tree = [table([LINK_TREE[v][d] for v in range(16)], col) for d in range(4)]
     depth = [table(TREE_DEPTH[t], col) for t in range(4)]
 
+    across = [mod4(x + k) * 4 + y for k in range(4)]
+    along = [x * 4 + mod4(y + k) for k in range(4)]
     barrier = pltpu.get_barrier_semaphore()
-    for d in range(4):
-        pl.semaphore_signal(barrier, inc=1, device_id=(row, neighbours[d]), device_id_type=MESH)
+    for k in range(1, 4):
+        pl.semaphore_signal(barrier, inc=1, device_id=(row, across[k]), device_id_type=MESH)
+        pl.semaphore_signal(barrier, inc=1, device_id=(row, along[k]), device_id_type=MESH)
     for r in (z_up, z_down, other):
         pl.semaphore_signal(barrier, inc=1, device_id=(r, col), device_id_type=MESH)
 
@@ -255,7 +275,7 @@
     def _():
         load_rows.start()
 
-    pl.semaphore_wait(barrier, 7)
+    pl.semaphore_wait(barrier, 9)
 
     @pl.when(top)
     def _():
@@ -301,11 +321,11 @@
     lead = core == 0
     q_depth = [z + core, mod4(4 - z) + core]
     q_next = [(z_up, lead & (z < 3)), (z_down, lead & (z != 1))]
-    c_depth = 6 + jnp.where(z == 2, 2, jnp.where(z == 0, 0, 1)) + core
+    c_depth = 1 + LAG * (5 + jnp.where(z == 2, 2, jnp.where(z == 0, 0, 1)) + core)
 
     def step(s, carry):
         for t in range(4):
-            i = s - depth[t]
+            i = s - LAG * depth[t]
 
             @pl.when((i >= 0) & (i < P_CHUNKS))
             def _(t=t, i=i):
@@ -326,7 +346,7 @@
                         p_copy(t, i, d).start()
 
         for h in range(2):
-            j = s - q_depth[h]
+            j = s - LAG * q_depth[h]
 
             @pl.when((j >= 0) & (j < Q_CHUNKS))
             def _(h=h, j=j):
@@ -366,13 +386,137 @@
 
         return carry
 
-    lax.fori_loop(0, P_CHUNKS + 6, step, 0)
+    lax.fori_loop(0, max(P_CHUNKS + 5 * LAG, C_CHUNKS + 1 + 8 * LAG), step, 0)
 
     @pl.when(top)
     def _():
         c_ref[0:256, :] = p_ref[0:256, 256:512]
         c_ref[256:512, :] = p_ref[256:512, 0:256]
 
+    inv0, inv1 = split(inv_ref[0]), split(inv_ref[1])
+    upper0 = q_ref[0:256, :]
+    ratio = dot_split(split(c_ref[256:512, :]), inv0)
+    u_ref[0:256, :] = upper0
+    u_ref[256:512, :] = q_ref[256:512, :] - dot(ratio, upper0)
+
+    @pl.when(source)
+    def _():
+        u_ref[0:256, 0:256] = jnp.zeros((256, 256), F32)
+        u_ref[256:512, 0:512] = jnp.zeros((256, 512), F32)
+
+    copy_u = pltpu.make_async_copy(u_ref, u_out, out_u)
+    copy_u.start()
+    us_ref[...] = dot(u_ref[...], s_ref[...])
+
+    rows = part.shape[0]
+    half = rows // 2
+    big = half // 4
+    small = big // 4
+    outer = (x, y)
+    inner = (y, x)
+    outer_peers = (across, along)
+    inner_peers = (along, across)
+
+    def at(start, count):
+        return pl.ds(pl.multiple_of(start, count), count)
+
+    def remote(src, dst, stage, h, k, peer):
+        return pltpu.make_async_remote_copy(
+            src_ref=src,
+            dst_ref=dst,
+            send_sem=send_i.at[stage, h, k - 1],
+            recv_sem=recv_i.at[stage, h, k - 1],
+            device_id=(row, peer),
+            device_id_type=MESH,
+        )
+
+    def first_copy(h, k):
+        to = mod4(jnp.where(h == 0, x, y) + k)
+        peer = jnp.where(h == 0, to * 4 + y, x * 4 + to)
+        return remote(part.at[at(h * half + to * big, big), :], stage1.at[h, k - 1], 0, h, k, peer)
+
+    def l_copy(j):
+        return pltpu.make_async_copy(l_ref.at[at(j * big, big), :], l_out.at[at(j * big, big), :], out_l.at[j])
+
+    def one_tile(n, carry):
+        h = lax.rem(n, 2)
+        k = table((2, 1, 3, 0), lax.div(n, 2))
+        j = h * 4 + mod4(jnp.where(h == 0, x, y) + k)
+        mine = at(j * big, big)
+        below0 = (row > 0) | (j > 0)
+        below1 = (row > 0) | (j > 1)
+        p0 = p_ref[mine, 0:256]
+        lower0 = jnp.where(below0, dot_split(split(p0), inv0), 0.0)
+        rest = p_ref[mine, 256:512] - dot(lower0, c_ref[0:256, :])
+        lower1 = jnp.where(below1, dot_split(split(rest), inv1), 0.0)
+        l_ref[mine, 0:256] = lower0
+        l_ref[mine, 256:512] = lower1
+        l_copy(j).start()
+        part[mine, :] = g_ref[mine, :] - dot(lower0, us_ref[0:256, :]) - dot(lower1, us_ref[256:512, :])
+
+        @pl.when(source)
+        def _():
+            change0 = jnp.where(below0, lower0 - p0, 0.0)
+            change1 = jnp.where(below1, lower1 - rest, 0.0)
+            part[mine, :] += dot(change0, s_ref[0:256, :]) + dot(change1, s_ref[256:512, :])
+
+        @pl.when(k > 0)
+        def _():
+            first_copy(h, k).start()
+
+        return carry
+
+    lax.fori_loop(0, 8, one_tile, 0)
+
+    order = (2, 1, 3)
+    second, third, fourth = [], [], []
+    for h in range(2):
+        for k in order:
+            first_copy(h, k).wait_recv()
+        total = part[at(h * half + outer[h] * big, big), :]
+        for k in range(1, 4):
+            total = total + stage1[h, k - 1]
+        stage1[h, 3] = total
+        for k in order:
+            to = mod4(inner[h] + k)
+            copy = remote(
+                stage1.at[h, 3, at(to * small, small), :], stage2.at[h, k - 1], 1, h, k, inner_peers[h][k]
+            )
+            copy.start()
+            second.append((h, copy))
+    for h in range(2):
+        for g, copy in second:
+            if g == h:
+                copy.wait_recv()
+        total = stage1[h, 3, at(inner[h] * small, small), :]
+        for k in range(1, 4):
+            total = total + stage2[h, k - 1]
+        mine = at(h * half + outer[h] * big + inner[h] * small, small)
+        img[mine, :] = total
+        for k in order:
+            copy = remote(img.at[mine, :], img.at[mine, :], 2, h, k, inner_peers[h][k])
+            copy.start()
+            third.append((h, copy))
+    for h in range(2):
+        for g, copy in third:
+            if g == h:
+                copy.wait_recv()
+        mine = at(h * half + outer[h] * big, big)
+        for k in order:
+            copy = remote(img.at[mine, :], img.at[mine, :], 3, h, k, outer_peers[h][k])
+            copy.start()
+            fourth.append((h, copy))
+    for _, copy in fourth:
+        copy.wait_recv()
+    for h in range(2):
+        for k in order:
+            first_copy(h, k).wait_send()
+    for _, copy in second + third + fourth:
+        copy.wait_send()
+    copy_u.wait()
+    for j in range(8):
+        l_copy(j).wait()
+
     def drain_p(i, carry):
         for d in range(4):
 
@@ -417,19 +561,30 @@
     lax.fori_loop(0, C_CHUNKS, drain_c, 0)
 
 
-def bcast(asm):
+def panels(asm, g, inverses, strokes):
     rows, cols = asm.shape
+    modes = strokes.shape[1]
     vmem = pl.BlockSpec(memory_space=VMEM)
+    hbm = pl.BlockSpec(memory_space=pl.ANY)
     return pl.pallas_call(
-        bcast_kernel,
+        panel_kernel,
         out_shape=(
             jax.ShapeDtypeStruct((rows, 512), F32),
             jax.ShapeDtypeStruct((512, cols), F32),
-            jax.ShapeDtypeStruct((512, 256), F32),
+            jax.ShapeDtypeStruct((rows, modes), F32),
         ),
-        in_specs=[pl.BlockSpec(memory_space=pl.ANY)],
-        out_specs=(vmem, vmem, vmem),
+        in_specs=[hbm, vmem, vmem, vmem],
+        out_specs=(hbm, hbm, vmem),
         scratch_shapes=[
+            VMEM((rows, 512), F32),
+            VMEM((512, cols), F32),
+            VMEM((512, 256), F32),
+            VMEM((rows, 512), F32),
+            VMEM((512, cols), F32),
+            VMEM((512, modes), F32),
+            VMEM((rows, modes), F32),
+            VMEM((2, 4, rows // 8, modes), F32),
+            VMEM((2, 3, rows // 32, modes), F32),
             DMA((4,)),
             DMA,
             DMA((4, P_CHUNKS)),
@@ -438,49 +593,42 @@
             DMA((2, Q_CHUNKS)),
             DMA((C_CHUNKS, 3)),
             DMA((C_CHUNKS,)),
+            DMA((8,)),
+            DMA,
+            DMA((4, 2, 3)),
+            DMA((4, 2, 3)),
         ],
         compiler_params=pltpu.CompilerParams(collective_id=1, has_side_effects=True),
-        name="bcast",
-    )(asm)
-
-
-def update_kernel(asm_ref, p_ref, q_ref, c_ref, inv_ref, s_ref, out_ref, img_ref, u_ref):
+        name="panels",
+    )(asm, g, inverses, strokes)
+
+
+def update_kernel(asm_ref, l_ref, u_ref, image_ref, out_ref, img_ref, u_high, u_low):
     i = pl.program_id(0)
     row = lax.axis_index("row")
-    first_col = lax.axis_index("col") == 0
 
     @pl.when(i == 0)
     def _():
-        ratio = dot(c_ref[256:512, :], inv_ref[0])
-        u_ref[0:256, :] = q_ref[0:256, :]
-        u_ref[256:512, :] = q_ref[256:512, :] - dot(ratio, q_ref[0:256, :])
-
-        @pl.when(first_col)
-        def _():
-            u_ref[0:256, 0:256] = jnp.zeros((256, 256), F32)
-            u_ref[256:512, 0:512] = jnp.zeros((256, 512), F32)
-
-    below0 = (row > 0) | (i > 0)
-    below1 = (row > 0) | (i > 1)
-    lower0 = jnp.where(below0, dot(p_ref[:, 0:256], inv_ref[0]), 0.0)
-    rest = p_ref[:, 256:512] - dot(lower0, c_ref[0:256, :])
-    lower1 = jnp.where(below1, dot(rest, inv_ref[1]), 0.0)
-    out_ref[...] = asm_ref[...] - dot(jnp.concatenate([lower0, lower1], axis=1), u_ref[...])
-
-    @pl.when(first_col)
+        u_high[...], u_low[...] = split(u_ref[...])
+
+    lower = l_ref[...]
+    out_ref[...] = asm_ref[...] - dot_split(split(lower), (u_high[...], u_low[...]))
+    img_ref[...] = image_ref[...]
+
+    @pl.when(lax.axis_index("col") == 0)
     def _():
-        out_ref[:, 0:256] = jnp.where(below0, lower0, asm_ref[:, 0:256])
-        out_ref[:, 256:512] = jnp.where(below1, lower1, rest)
-
-    img_ref[...] = dot(out_ref[...], s_ref[...])
-
-
-def update(asm, p, q, c, inverses, strokes):
+        @pl.when((row > 0) | (i > 0))
+        def _():
+            out_ref[:, 0:256] = lower[:, 0:256]
+
+        @pl.when((row > 0) | (i > 1))
+        def _():
+            out_ref[:, 256:512] = lower[:, 256:512]
+
+
+def update(asm, lower, upper, image):
     rows, cols = asm.shape
     size = 256
-
-    def whole(shape):
-        return pl.BlockSpec(shape, lambda i: (0,) * len(shape))
 
     def tiles(width):
         return pl.BlockSpec((size, width), lambda i: (i, 0))
@@ -490,138 +638,27 @@
         grid=(rows // size,),
         out_shape=(
             jax.ShapeDtypeStruct((rows, cols), F32),
-            jax.ShapeDtypeStruct((rows, strokes.shape[1]), F32),
+            jax.ShapeDtypeStruct(image.shape, F32),
         ),
         in_specs=[
             tiles(cols),
             tiles(512),
-            whole(q.shape),
-            whole(c.shape),
-            whole(inverses.shape),
-            whole(strokes.shape),
+            pl.BlockSpec(upper.shape, lambda i: (0, 0)),
+            tiles(image.shape[1]),
         ],
-        out_specs=(tiles(cols), tiles(strokes.shape[1])),
-        scratch_shapes=[VMEM((512, cols), F32)],
+        out_specs=(tiles(cols), tiles(image.shape[1])),
+        scratch_shapes=[VMEM(upper.shape, jnp.bfloat16), VMEM(upper.shape, jnp.bfloat16)],
         name="update",
-    )(asm, p, q, c, inverses, strokes)
-
-
-def image_kernel(part, out, stage1, stage2, send_sem, recv_sem):
-    row = lax.axis_index("row")
-    col = lax.axis_index("col")
-    x, y = lax.div(col, 4), lax.rem(col, 4)
-    rows = part.shape[0]
-    half = rows // 2
-    big = half // 4
-    small = big // 4
-    across = [mod4(x + k) * 4 + y for k in range(4)]
-    along = [x * 4 + mod4(y + k) for k in range(4)]
-
-    barrier = pltpu.get_barrier_semaphore()
-    for k in range(1, 4):
-        pl.semaphore_signal(barrier, inc=1, device_id=(row, across[k]), device_id_type=MESH)
-        pl.semaphore_signal(barrier, inc=1, device_id=(row, along[k]), device_id_type=MESH)
-    pl.semaphore_wait(barrier, 6)
-
-    outer = (x, y)
-    inner = (y, x)
-    outer_peers = (across, along)
-    inner_peers = (along, across)
-
-    def remote(src, dst, stage, h, k, peer):
-        return pltpu.make_async_remote_copy(
-            src_ref=src,
-            dst_ref=dst,
-            send_sem=send_sem.at[stage, h, k - 1],
-            recv_sem=recv_sem.at[stage, h, k - 1],
-            device_id=(row, peer),
-            device_id_type=MESH,
-        )
-
-    def rows_at(start, count):
-        return pl.ds(pl.multiple_of(start, count), count)
-
-    order = (2, 1, 3)
-    first, second, third, fourth = [], [], [], []
-    for k in order:
-        for h in range(2):
-            to = mod4(outer[h] + k)
-            copy = remote(
-                part.at[rows_at(h * half + to * big, big), :], stage1.at[h, k - 1], 0, h, k, outer_peers[h][k]
-            )
-            copy.start()
-            first.append((h, copy))
-    for h in range(2):
-        for g, copy in first:
-            if g == h:
-                copy.wait_recv()
-        total = part[rows_at(h * half + outer[h] * big, big), :]
-        for k in range(1, 4):
-            total = total + stage1[h, k - 1]
-        stage1[h, 3] = total
-        for k in order:
-            to = mod4(inner[h] + k)
-            copy = remote(
-                stage1.at[h, 3, rows_at(to * small, small), :], stage2.at[h, k - 1], 1, h, k, inner_peers[h][k]
-            )
-            copy.start()
-            second.append((h, copy))
-    for h in range(2):
-        for g, copy in second:
-            if g == h:
-                copy.wait_recv()
-        total = stage1[h, 3, rows_at(inner[h] * small, small), :]
-        for k in range(1, 4):
-            total = total + stage2[h, k - 1]
-        mine = rows_at(h * half + outer[h] * big + inner[h] * small, small)
-        out[mine, :] = total
-        for k in order:
-            copy = remote(out.at[mine, :], out.at[mine, :], 2, h, k, inner_peers[h][k])
-            copy.start()
-            third.append((h, copy))
-    for h in range(2):
-        for g, copy in third:
-            if g == h:
-                copy.wait_recv()
-        mine = rows_at(h * half + outer[h] * big, big)
-        for k in order:
-            copy = remote(out.at[mine, :], out.at[mine, :], 3, h, k, outer_peers[h][k])
-            copy.start()
-            fourth.append((h, copy))
-    for _, copy in fourth:
-        copy.wait_recv()
-    for _, copy in first + second + third + fourth:
-        copy.wait_send()
-
-
-def image_sum(part):
-    rows, cols = part.shape
-    vmem = pl.BlockSpec(memory_space=VMEM)
-    return pl.pallas_call(
-        image_kernel,
-        out_shape=jax.ShapeDtypeStruct(part.shape, F32),
-        in_specs=[vmem],
-        out_specs=vmem,
-        scratch_shapes=[
-            VMEM((2, 4, rows // 8, cols), F32),
-            VMEM((2, 3, rows // 32, cols), F32),
-            DMA((4, 2, 3)),
-            DMA((4, 2, 3)),
-        ],
-        compiler_params=pltpu.CompilerParams(collective_id=2, has_side_effects=True),
-        name="image_sum",
-    )(part)
+    )(asm, lower, upper, image)
 
 
 def on_device(far_field, inverses, test_table, trial_table, tile_list, tile_nodes, strokes):
     packed = make_pieces(tile_list, tile_nodes, test_table, trial_table, 16)
     arrived = exchange(packed)
     labels = arrived[:, 256:258, 0].astype(jnp.int32).reshape(32)
-    asm = place(labels, far_field, arrived)
-    p, q, c = bcast(asm)
-    factored, part = update(asm, p, q, c, inverses, strokes)
-    image = image_sum(part)
-    return factored, image
+    asm, g = place(labels, far_field, arrived, strokes)
+    lower, upper, image = panels(asm, g, inverses, strokes)
+    return update(asm, lower, upper, image)
 
 
 def solution(mesh):

time: 249 us -> 181 us (0.73)
  Pallas kernels: 240 us -> 175 us
  local copies, waits for them, and re-layouts: 5.01 us -> 1.96 us
    pallas_call x3 -> x2, Pallas kernels: 166 us -> 113 us  [the longest x1 94.6 us: panels(): pl.pallas_call(panel_kernel, out_shape=(jax.ShapeDtypeStruct((rows, 512),...]
    pallas_call x1, Pallas kernels: 26.5 us -> 14.8 us  [update(): pl.pallas_call(update_kernel, grid=(rows // size,), out_shape=(jax.ShapeD...]
    unnamed x2 -> x1, local copies, waits for them, and re-layouts: 4.4 us -> 1.35 us
where the time goes in v2:
time: 181 us; the launch traced here: 179 us
  Pallas kernels  175 us (97%)
  local copies, waits for them, and re-layouts  1.96 us (1%)
    pallas_call x1, Pallas kernels, panels(): pl.pallas_call(panel_kernel, out_shape=(jax.ShapeDtypeStruct((rows, 512),...  94.6 us
    pallas_call x1, Pallas kernels, exchange(): pl.pallas_call(exchange_kernel, out_shape=jax.ShapeDtypeStruct(packed.sha...  32.7 us
    pallas_call x1, Pallas kernels, place(): pl.pallas_call(place_kernel, out_shape=(jax.ShapeDtypeStruct(far.shape, F...  18.7 us
    pallas_call x1, Pallas kernels, update(): pl.pallas_call(update_kernel, grid=(rows // size,), out_shape=(jax.ShapeD...  14.8 us
    pallas_call x1, Pallas kernels, make_pieces(): pl.pallas_call(pieces_kernel, out_shape=jax.ShapeDtypeStruct((dests, 2 *...  14.7 us

profile of v2, /device:TPU:72, one launch (start us, length us, event | category | flops | bytes accessed | tf_op | source)
XLA Modules:
  0.0 179.2 jit_solution(5691630023297894944)
XLA Ops:
  0.6 1.4 copy.10.tiles_ref
  2.0 14.7 %pieces.1.packed = f32[16,264,128]{2,1,0:T(8,128)} custom-call(s32[16,2]{1,0:T(8,128)} %copy.10.tiles_ref, s32[16,256]{1,0:T(8,128)} %nodes_ref.1, f32[4096,128]{1,0:T(8,128)} %test_ref.1, f32[4096,128]{1,0:T(8,128)} %trial_ref.1), custom_call_target="tpu_custom_call" | custom-call | tf_op jit(solution)/shard_map/pieces/pallas_call | solution.py:97
  16.7 32.7 %exchange.1.arrived = f32[16,264,128]{2,1,0:T(8,128)} custom-call(f32[16,264,128]{2,1,0:T(8,128)} %pieces.1.packed), custom_call_target="tpu_custom_call" | custom-call | tf_op jit(solution)/shard_map/exchange/pallas_call | solution.py:154
  49.4 1.2 convert_reduce_fusion
  50.6 0.6 convert_element_type.8.label_ref
  51.2 18.7 %place.1 = (f32[2048,1024]{1,0:T(8,128)}, f32[2048,256]{1,0:T(8,128)}) custom-call(s32[32]{0:T(128)} %convert_element_type.8.label_ref, f32[2048,1024]{1,0:T(8,128)} %far.1, f32[16,264,128]{2,1,0:T(8,128)} %exchange.1.arrived, f32[1024,256]{1,0:T(8,128)} %s_ref.3), custom_call_target="tpu_custom_call" | custom-call | tf_op jit(solution)/shard_map/place/pallas_call | solution.py:208
  69.8 94.6 %panels.1 = (f32[2048,512]{1,0:T(8,128)}, f32[512,1024]{1,0:T(8,128)}, f32[2048,256]{1,0:T(8,128)}) custom-call(f32[2048,1024]{1,0:T(8,128)} %get-tuple-element.7.asm.asm_ref, f32[2048,256]{1,0:T(8,128)} %get-tuple-element.8.g_ref, f32[2,256,256]{2,1,0:T(8,128)} %inv_ref.1, f32[1024,256]{1,0:T(8,128)} %s_ref.3), custom_call_target="tpu_custom_call" | custom-call | tf_op jit(solution)/shard_map/panels/pallas_call | solution.py:569
  164.4 14.8 %update.1 = (f32[2048,1024]{1,0:T(8,128)}, f32[2048,256]{1,0:T(8,128)}) custom-call(f32[2048,1024]{1,0:T(8,128)} %get-tuple-element.7.asm.asm_ref, f32[2048,512]{1,0:T(8,128)} %get-tuple-element.9.l_ref, f32[512,1024]{1,0:T(8,128)} %get-tuple-element.10.u_ref, f32[2048,256]{1,0:T(8,128)} %get-tuple-element.11.image_ref), custom_call_target="tpu_custom_call" | custom-call | tf_op jit(solution)/shard_map/update/pallas_call | solution.py:636

commit v3 on v2

--- a/solution.py
+++ b/solution.py
@@ -96,7 +96,7 @@
     quad = tile_nodes.shape[1]
     return pl.pallas_call(
         pieces_kernel,
-        out_shape=jax.ShapeDtypeStruct((dests, 2 * tile + 8, tile), F32),
+        out_shape=VMEM((dests, 2 * tile + 8, tile), F32),
         in_specs=[
             pl.BlockSpec(memory_space=pltpu.SMEM),
             pl.BlockSpec(memory_space=pltpu.SMEM),
@@ -110,17 +110,23 @@
             pltpu.SMEM((dests,), jnp.int32),
             pltpu.SMEM((2 * dests,), jnp.int32),
         ],
+        compiler_params=pltpu.CompilerParams(vmem_limit_bytes=8 << 20),
         name="pieces",
     )(tile_list, tile_nodes, test_table, trial_table)
 
 
 OFFSETS = sorted(
     ((dx, dy) for dx in range(4) for dy in range(4) if dx or dy),
-    key=lambda o: -(min(o[0], 4 - o[0]) + min(o[1], 4 - o[1])),
+    key=lambda o: min(o[0], 4 - o[0]) + min(o[1], 4 - o[1]),
 )
-
-
-def exchange_kernel(packed, arrived, send_sem, recv_sem, own_sem):
+FAR_PARTS = 8
+
+
+def resident(array):
+    return pltpu.with_memory_space_constraint(array, VMEM)
+
+
+def exchange_kernel(packed, far_hbm, s_hbm, arrived, far, g, strokes, send_sem, recv_sem, own_sem, far_sem, s_sem):
     row = lax.axis_index("row")
     col = lax.axis_index("col")
     x, y = lax.div(col, 4), lax.rem(col, 4)
@@ -128,8 +134,15 @@
     barrier = pltpu.get_barrier_semaphore()
     for peer in peers:
         pl.semaphore_signal(barrier, inc=1, device_id=(row, peer), device_id_type=MESH)
+    size = far.shape[0] // FAR_PARTS
+    load_s = pltpu.make_async_copy(s_hbm, strokes, s_sem)
+    load_s.start()
+    loads = []
+    for j in range(FAR_PARTS):
+        part = pl.ds(j * size, size)
+        loads.append(pltpu.make_async_copy(far_hbm.at[part], far.at[part], far_sem.at[j]))
+        loads[-1].start()
     pl.semaphore_wait(barrier, len(peers))
-    own = pltpu.make_async_copy(packed.at[col], arrived.at[col], own_sem)
     copies = []
     for k, peer in enumerate(peers):
         copies.append(
@@ -143,84 +156,80 @@
             )
         )
         copies[-1].start()
+    own = pltpu.make_async_copy(packed.at[col], arrived.at[col], own_sem)
     own.start()
+    load_s.wait()
+    both = split(strokes[...])
+    for j in range(FAR_PARTS):
+        loads[j].wait()
+        part = pl.ds(j * size, size)
+        g[part, :] = dot_split(split(far[part, :]), both)
     own.wait()
     for copy in copies:
         copy.wait()
 
 
-def exchange(packed):
+def exchange(packed, far, strokes):
     n = len(OFFSETS)
+    hbm = pl.BlockSpec(memory_space=pltpu.HBM)
+    vmem = pl.BlockSpec(memory_space=VMEM)
     return pl.pallas_call(
         exchange_kernel,
-        out_shape=jax.ShapeDtypeStruct(packed.shape, F32),
-        in_specs=[pl.BlockSpec(memory_space=VMEM)],
-        out_specs=pl.BlockSpec(memory_space=pl.ANY),
-        scratch_shapes=[DMA((n,)), DMA((n,)), DMA],
-        compiler_params=pltpu.CompilerParams(collective_id=0, has_side_effects=True),
+        out_shape=(
+            VMEM(packed.shape, F32),
+            VMEM(far.shape, F32),
+            VMEM((far.shape[0], strokes.shape[1]), F32),
+            VMEM(strokes.shape, F32),
+        ),
+        in_specs=[vmem, hbm, hbm],
+        out_specs=(vmem,) * 4,
+        scratch_shapes=[DMA((n,)), DMA((n,)), DMA, DMA((FAR_PARTS,)), DMA],
+        compiler_params=pltpu.CompilerParams(
+            collective_id=0, has_side_effects=True, vmem_limit_bytes=8 << 20
+        ),
         name="exchange",
-    )(packed)
-
-
-def place_kernel(label_ref, far, arrived, s_ref, out, g_ref, block, tiles, in_sem, out_sem, tile_sem):
-    rows, cols = block.shape
-    chunks = 8
-    size = rows // chunks
-    tile = tiles.shape[2]
-    bring = pltpu.make_async_copy(arrived, tiles, tile_sem)
-    bring.start()
-
-    def part(j):
-        return pl.ds(j * size, size)
-
-    ins = [pltpu.make_async_copy(far.at[part(j)], block.at[part(j)], in_sem.at[j]) for j in range(chunks)]
-    outs = [pltpu.make_async_copy(block.at[part(j)], out.at[part(j)], out_sem.at[j]) for j in range(chunks)]
-    for copy in ins:
-        copy.start()
-    strokes = split(s_ref[...])
-    bring.wait()
-    for j in range(chunks):
-        ins[j].wait()
-
-        def add(s, carry):
-            lab = label_ref[s]
-
-            @pl.when((lab >= 0) & (lax.div(lab, 16) == j))
-            def _():
-                at = (
-                    pl.ds(pl.multiple_of(lax.div(lab, 8) * tile, tile), tile),
-                    pl.ds(pl.multiple_of(lax.rem(lab, 8) * tile, tile), tile),
-                )
-                piece = tiles[lax.div(s, 2), pl.ds(pl.multiple_of(lax.rem(s, 2) * tile, tile), tile), :]
-                block[at] = block[at] + piece
-
-            return carry
-
-        lax.fori_loop(0, label_ref.shape[0], add, 0)
-        outs[j].start()
-        g_ref[part(j), :] = dot_split(split(block[part(j), :]), strokes)
-    for copy in outs:
-        copy.wait()
-
-
-def place(labels, far, arrived, strokes):
-    rows = far.shape[0]
+    )(
+        resident(packed),
+        pltpu.with_memory_space_constraint(far, pltpu.HBM),
+        pltpu.with_memory_space_constraint(strokes, pltpu.HBM),
+    )
+
+
+def place_kernel(arrived, far, g0, strokes, out, g, label):
+    tile = arrived.shape[2]
+    for d in range(arrived.shape[0]):
+        for k in range(2):
+            at = 2 * tile + k
+            label[2 * d + k] = jnp.max(arrived[d, at : at + 1, :]).astype(jnp.int32)
+
+    def add(s, carry):
+        lab = label[s]
+
+        @pl.when(lab >= 0)
+        def _():
+            rows = pl.ds(pl.multiple_of(lax.div(lab, 8) * tile, tile), tile)
+            cols = pl.ds(pl.multiple_of(lax.rem(lab, 8) * tile, tile), tile)
+            piece = arrived[lax.div(s, 2), pl.ds(pl.multiple_of(lax.rem(s, 2) * tile, tile), tile), :]
+            out[rows, cols] = out[rows, cols] + piece
+            g[rows, :] = g[rows, :] + dot(piece, strokes[cols, :])
+
+        return carry
+
+    lax.fori_loop(0, label.shape[0], add, 0)
+
+
+def place(arrived, far, g, strokes):
+    vmem = pl.BlockSpec(memory_space=VMEM)
     return pl.pallas_call(
         place_kernel,
-        out_shape=(
-            jax.ShapeDtypeStruct(far.shape, F32),
-            jax.ShapeDtypeStruct((rows, strokes.shape[1]), F32),
-        ),
-        in_specs=[
-            pl.BlockSpec(memory_space=pltpu.SMEM),
-            pl.BlockSpec(memory_space=pl.ANY),
-            pl.BlockSpec(memory_space=pl.ANY),
-            pl.BlockSpec(memory_space=VMEM),
-        ],
-        out_specs=(pl.BlockSpec(memory_space=pl.ANY), pl.BlockSpec(memory_space=VMEM)),
-        scratch_shapes=[VMEM(far.shape, F32), VMEM(arrived.shape, F32), DMA((8,)), DMA((8,)), DMA],
+        out_shape=(VMEM(far.shape, F32), VMEM(g.shape, F32)),
+        in_specs=[vmem] * 4,
+        out_specs=(vmem, vmem),
+        scratch_shapes=[pltpu.SMEM((2 * arrived.shape[0],), jnp.int32)],
+        input_output_aliases={1: 0, 2: 1},
+        compiler_params=pltpu.CompilerParams(vmem_limit_bytes=8 << 20),
         name="place",
-    )(labels, far, arrived, strokes)
+    )(resident(arrived), resident(far), resident(g), resident(strokes))
 
 
 P_CHUNKS = 32
@@ -232,9 +241,8 @@
 
 
 def panel_kernel(
-    asm, g_ref, inv_ref, s_ref, l_out, u_out, img, p_ref, q_ref, c_ref, l_ref, u_ref, us_ref, part,
-    stage1, stage2, load_p, load_q, send_p, recv_p, send_q, recv_q, send_c, recv_c, out_l, out_u,
-    send_i, recv_i
+    asm, g_ref, inv_ref, s_ref, out_ref, img, p_ref, q_ref, c_ref, l_ref, u_ref, u_high, u_low, us_ref,
+    part, stage1, stage2, load_p, load_q, send_p, recv_p, send_q, recv_q, send_c, recv_c, send_i, recv_i
 ):
     row = lax.axis_index("row")
     col = lax.axis_index("col")
@@ -404,9 +412,8 @@
         u_ref[0:256, 0:256] = jnp.zeros((256, 256), F32)
         u_ref[256:512, 0:512] = jnp.zeros((256, 512), F32)
 
-    copy_u = pltpu.make_async_copy(u_ref, u_out, out_u)
-    copy_u.start()
-    us_ref[...] = dot(u_ref[...], s_ref[...])
+    u_high[...], u_low[...] = split(u_ref[...])
+    us_ref[...] = dot_split((u_high[...], u_low[...]), split(s_ref[...]))
 
     rows = part.shape[0]
     half = rows // 2
@@ -435,8 +442,20 @@
         peer = jnp.where(h == 0, to * 4 + y, x * 4 + to)
         return remote(part.at[at(h * half + to * big, big), :], stage1.at[h, k - 1], 0, h, k, peer)
 
-    def l_copy(j):
-        return pltpu.make_async_copy(l_ref.at[at(j * big, big), :], l_out.at[at(j * big, big), :], out_l.at[j])
+    def finish_tile(j, carry):
+        mine = at(j * big, big)
+        lower = l_ref[mine, :]
+        out_ref[mine, :] = asm[mine, :] - dot_split(split(lower), (u_high[...], u_low[...]))
+
+        @pl.when(source & ((row > 0) | (j > 0)))
+        def _():
+            out_ref[mine, 0:256] = l_ref[mine, 0:256]
+
+        @pl.when(source & ((row > 0) | (j > 1)))
+        def _():
+            out_ref[mine, 256:512] = l_ref[mine, 256:512]
+
+        return carry
 
     def one_tile(n, carry):
         h = lax.rem(n, 2)
@@ -451,7 +470,6 @@
         lower1 = jnp.where(below1, dot_split(split(rest), inv1), 0.0)
         l_ref[mine, 0:256] = lower0
         l_ref[mine, 256:512] = lower1
-        l_copy(j).start()
         part[mine, :] = g_ref[mine, :] - dot(lower0, us_ref[0:256, :]) - dot(lower1, us_ref[256:512, :])
 
         @pl.when(source)
@@ -484,6 +502,7 @@
             )
             copy.start()
             second.append((h, copy))
+    lax.fori_loop(0, 2, finish_tile, 0)
     for h in range(2):
         for g, copy in second:
             if g == h:
@@ -497,6 +516,7 @@
             copy = remote(img.at[mine, :], img.at[mine, :], 2, h, k, inner_peers[h][k])
             copy.start()
             third.append((h, copy))
+    lax.fori_loop(2, 4, finish_tile, 0)
     for h in range(2):
         for g, copy in third:
             if g == h:
@@ -506,6 +526,7 @@
             copy = remote(img.at[mine, :], img.at[mine, :], 3, h, k, outer_peers[h][k])
             copy.start()
             fourth.append((h, copy))
+    lax.fori_loop(4, 8, finish_tile, 0)
     for _, copy in fourth:
         copy.wait_recv()
     for h in range(2):
@@ -513,10 +534,6 @@
             first_copy(h, k).wait_send()
     for _, copy in second + third + fourth:
         copy.wait_send()
-    copy_u.wait()
-    for j in range(8):
-        l_copy(j).wait()
-
     def drain_p(i, carry):
         for d in range(4):
 
@@ -565,22 +582,19 @@
     rows, cols = asm.shape
     modes = strokes.shape[1]
     vmem = pl.BlockSpec(memory_space=VMEM)
-    hbm = pl.BlockSpec(memory_space=pl.ANY)
     return pl.pallas_call(
         panel_kernel,
-        out_shape=(
-            jax.ShapeDtypeStruct((rows, 512), F32),
-            jax.ShapeDtypeStruct((512, cols), F32),
-            jax.ShapeDtypeStruct((rows, modes), F32),
-        ),
-        in_specs=[hbm, vmem, vmem, vmem],
-        out_specs=(hbm, hbm, vmem),
+        out_shape=(VMEM((rows, cols), F32), VMEM((rows, modes), F32)),
+        in_specs=[vmem] * 4,
+        out_specs=(vmem, vmem),
         scratch_shapes=[
             VMEM((rows, 512), F32),
             VMEM((512, cols), F32),
             VMEM((512, 256), F32),
             VMEM((rows, 512), F32),
             VMEM((512, cols), F32),
+            VMEM((512, cols), jnp.bfloat16),
+            VMEM((512, cols), jnp.bfloat16),
             VMEM((512, modes), F32),
             VMEM((rows, modes), F32),
             VMEM((2, 4, rows // 8, modes), F32),
@@ -593,72 +607,21 @@
             DMA((2, Q_CHUNKS)),
             DMA((C_CHUNKS, 3)),
             DMA((C_CHUNKS,)),
-            DMA((8,)),
-            DMA,
             DMA((4, 2, 3)),
             DMA((4, 2, 3)),
         ],
-        compiler_params=pltpu.CompilerParams(collective_id=1, has_side_effects=True),
+        compiler_params=pltpu.CompilerParams(
+            collective_id=1, has_side_effects=True, vmem_limit_bytes=32 << 20
+        ),
         name="panels",
-    )(asm, g, inverses, strokes)
-
-
-def update_kernel(asm_ref, l_ref, u_ref, image_ref, out_ref, img_ref, u_high, u_low):
-    i = pl.program_id(0)
-    row = lax.axis_index("row")
-
-    @pl.when(i == 0)
-    def _():
-        u_high[...], u_low[...] = split(u_ref[...])
-
-    lower = l_ref[...]
-    out_ref[...] = asm_ref[...] - dot_split(split(lower), (u_high[...], u_low[...]))
-    img_ref[...] = image_ref[...]
-
-    @pl.when(lax.axis_index("col") == 0)
-    def _():
-        @pl.when((row > 0) | (i > 0))
-        def _():
-            out_ref[:, 0:256] = lower[:, 0:256]
-
-        @pl.when((row > 0) | (i > 1))
-        def _():
-            out_ref[:, 256:512] = lower[:, 256:512]
-
-
-def update(asm, lower, upper, image):
-    rows, cols = asm.shape
-    size = 256
-
-    def tiles(width):
-        return pl.BlockSpec((size, width), lambda i: (i, 0))
-
-    return pl.pallas_call(
-        update_kernel,
-        grid=(rows // size,),
-        out_shape=(
-            jax.ShapeDtypeStruct((rows, cols), F32),
-            jax.ShapeDtypeStruct(image.shape, F32),
-        ),
-        in_specs=[
-            tiles(cols),
-            tiles(512),
-            pl.BlockSpec(upper.shape, lambda i: (0, 0)),
-            tiles(image.shape[1]),
-        ],
-        out_specs=(tiles(cols), tiles(image.shape[1])),
-        scratch_shapes=[VMEM(upper.shape, jnp.bfloat16), VMEM(upper.shape, jnp.bfloat16)],
-        name="update",
-    )(asm, lower, upper, image)
+    )(resident(asm), resident(g), inverses, resident(strokes))
 
 
 def on_device(far_field, inverses, test_table, trial_table, tile_list, tile_nodes, strokes):
     packed = make_pieces(tile_list, tile_nodes, test_table, trial_table, 16)
-    arrived = exchange(packed)
-    labels = arrived[:, 256:258, 0].astype(jnp.int32).reshape(32)
-    asm, g = place(labels, far_field, arrived, strokes)
-    lower, upper, image = panels(asm, g, inverses, strokes)
-    return update(asm, lower, upper, image)
+    arrived, far, g, held_strokes = exchange(packed, far_field, strokes)
+    asm, g = place(arrived, far, g, held_strokes)
+    return panels(asm, g, inverses, held_strokes)
 
 
 def solution(mesh):

time: 181 us -> 149 us (0.82)
  Pallas kernels: 175 us -> 138 us
  local copies, waits for them, and re-layouts: 1.96 us -> 9.38 us
    pallas_call x5 -> x4, Pallas kernels: 175 us -> 138 us  [the longest x1 89.8 us: panels(): pl.pallas_call(panel_kernel, out_shape=(VMEM((rows, cols), F32), VMEM((ro...]
    unnamed x1 -> x11, local copies, waits for them, and re-layouts: 1.35 us -> 9.38 us
where the time goes in v3:
time: 149 us; the launch traced here: 148 us
  Pallas kernels  138 us (93%)
  local copies, waits for them, and re-layouts  9.38 us (6%)
    pallas_call x1, Pallas kernels, panels(): pl.pallas_call(panel_kernel, out_shape=(VMEM((rows, cols), F32), VMEM((ro...  89.8 us
    pallas_call x1, Pallas kernels, exchange(): pl.pallas_call(exchange_kernel, out_shape=(VMEM(packed.shape, F32), VMEM(...  32.3 us
    pallas_call x1, Pallas kernels, make_pieces(): pl.pallas_call(pieces_kernel, out_shape=VMEM((dests, 2 * tile + 8, tile),...  12.8 us
    unnamed x11, local copies, waits for them, and re-layouts  9.38 us

profile of v3, /device:TPU:72, one launch (start us, length us, event | category | flops | bytes accessed | tf_op | source)
XLA Modules:
  0.0 147.9 jit_solution(2277249122412449809)
XLA Ops:
  0.6 0.8 copy.11.tiles_ref
  1.4 0.0 copy-start
  1.4 1.6 %copy-done = f32[4096,128]{1,0:T(8,128)S(1)} copy-done((f32[4096,128]{1,0:T(8,128)S(1)}, f32[4096,128]{1,0:T(8,128)}, u32[]{:S(2)}) %copy-start) | copy-done | bytes 2097176
  3.0 0.0 copy-start.1
  3.0 1.6 %copy-done.1 = f32[4096,128]{1,0:T(8,128)S(1)} copy-done((f32[4096,128]{1,0:T(8,128)S(1)}, f32[4096,128]{1,0:T(8,128)}, u32[]{:S(2)}) %copy-start.1) | copy-done | bytes 2097176
  4.6 0.0 copy-start.3
  4.6 0.7 copy-done.3
  5.3 12.8 %pieces.1.packed = f32[16,264,128]{2,1,0:T(8,128)S(1)} custom-call(s32[16,2]{1,0:T(8,128)S(1)} %copy.11.tiles_ref, s32[16,256]{1,0:T(8,128)S(1)} %copy-done.3, f32[4096,128]{1,0:T(8,128)S(1)} %copy-done, f32[4096,128]{1,0:T(8,128)S(1)} %copy-done.1), custom_call_target="tpu_custom_call" | custom-call | tf_op jit(solution)/shard_map/pieces/pallas_call | solution.py:97
  18.1 32.3 %exchange.1 = (f32[16,264,128]{2,1,0:T(8,128)S(1)}, f32[2048,1024]{1,0:T(8,128)S(1)}, f32[2048,256]{1,0:T(8,128)S(1)}, f32[1024,256]{1,0:T(8,128)S(1)}) custom-call(f32[16,264,128]{2,1,0:T(8,128)S(1)} %pieces.1.packed, f32[2048,1024]{1,0:T(8,128)} %far_hbm.1, f32[1024,256]{1,0:T(8,128)} %s_hbm.1), custom_call_target="tpu_custom_call" | custom-call | tf_op jit(solution)/shard_map/exchange/pallas_call | solution.py:176
  50.4 0.0 copy-start.2
  50.4 2.9 %place.1 = (f32[2048,1024]{1,0:T(8,128)S(1)}, f32[2048,256]{1,0:T(8,128)S(1)}) custom-call(f32[16,264,128]{2,1,0:T(8,128)S(1)} %get-tuple-element.8.arrived, f32[2048,1024]{1,0:T(8,128)S(1)} %get-tuple-element.9.far, f32[2048,256]{1,0:T(8,128)S(1)} %get-tuple-element.10.g0, ...), custom_call_target="tpu_custom_call", output_to_operand_aliasing={{0}: (1, {}), {1}: (2, {})} | custom-call | tf_op jit(solution)/shard_map/place/pallas_call | solution.py:223
  53.3 0.0 copy-done.2
  53.3 89.8 %panels.1 = (f32[2048,1024]{1,0:T(8,128)S(1)}, f32[2048,256]{1,0:T(8,128)S(1)}) custom-call(f32[2048,1024]{1,0:T(8,128)S(1)} %get-tuple-element.12.asm, f32[2048,256]{1,0:T(8,128)S(1)} %get-tuple-element.13.g_ref, f32[2,256,256]{2,1,0:T(8,128)S(1)} %copy-done.2, f32[1024,256]{1,0:T(8,128)S(1)} %get-tuple-element.11.strokes.s_ref), custom_call_target="tpu_custom_call" | custom-call | tf_op jit(solution)/shard_map/panels/pallas_call | solution.py:585
  143.2 3.4 %copy.16 = f32[2048,1024]{1,0:T(8,128)} copy(f32[2048,1024]{1,0:T(8,128)S(1)} %get-tuple-element.14) | data formatting | bytes 16777216
  146.6 1.3 copy.17
Async XLA Ops:
  1.4 1.6 %copy-start = (f32[4096,128]{1,0:T(8,128)S(1)}, f32[4096,128]{1,0:T(8,128)}, u32[]{:S(2)}) copy-start(f32[4096,128]{1,0:T(8,128)} %test_ref.1) | copy-start | bytes 6291460
  3.0 1.6 %copy-start.1 = (f32[4096,128]{1,0:T(8,128)S(1)}, f32[4096,128]{1,0:T(8,128)}, u32[]{:S(2)}) copy-start(f32[4096,128]{1,0:T(8,128)} %trial_ref.1) | copy-start | bytes 6291460
  4.6 0.7 copy-start.3
  50.4 2.9 %copy-start.2 = (f32[2,256,256]{2,1,0:T(8,128)S(1)}, f32[2,256,256]{2,1,0:T(8,128)}, u32[]{:S(2)}) copy-start(f32[2,256,256]{2,1,0:T(8,128)} %inv_ref.1) | copy-start | bytes 1572868

commit v4 on v3

--- a/solution.py
+++ b/solution.py
@@ -54,12 +54,23 @@
     return dot_split(split(a), split(b))
 
 
-def pieces_kernel(tiles_ref, nodes_ref, test_ref, trial_ref, out_ref, left, right, count, label):
+def pieces_kernel(
+    tiles_hbm, nodes_hbm, test_hbm, trial_hbm, out_ref, test_ref, trial_ref, left, right, tiles_ref, nodes_ref,
+    count, label, sem
+):
     owned, quad = nodes_ref.shape
     dests = out_ref.shape[0]
     tile = test_ref.shape[1]
     block_cols = 8
     block_rows = 16
+    loads = [
+        pltpu.make_async_copy(src, dst, sem.at[n])
+        for n, (src, dst) in enumerate(
+            ((tiles_hbm, tiles_ref), (nodes_hbm, nodes_ref), (test_hbm, test_ref), (trial_hbm, trial_ref))
+        )
+    ]
+    for load in loads:
+        load.start()
 
     def clear(at, carry):
         count[at] = 0
@@ -68,24 +79,42 @@
         return carry
 
     lax.fori_loop(0, dests, clear, 0)
-
-    def one_tile(t, carry):
-        for q in range(quad):
-            node = nodes_ref[t, q]
-            left[pl.ds(q, 1), :] = test_ref[pl.ds(node, 1), :]
-            right[pl.ds(q, 1), :] = trial_ref[pl.ds(node, 1), :]
-        piece = dot(left[...].T, right[...])
-        block_row = lax.rem(tiles_ref[t, 0], block_rows)
-        block_col = tiles_ref[t, 1]
+    for load in loads:
+        load.wait()
+    sublane = lax.broadcasted_iota(jnp.int32, (8, tile), 0)
+
+    def gather(t, slot):
+        for q in range(0, quad, 8):
+            nodes = [nodes_ref[t, q + k] for k in range(8)]
+            for table_ref, to in ((test_ref, left), (trial_ref, right)):
+                rows = [jnp.broadcast_to(table_ref[pl.ds(node, 1), :], (8, tile)) for node in nodes]
+                for width in (1, 2, 4):
+                    mask = lax.rem(sublane, 2 * width) < width
+                    rows = [jnp.where(mask, rows[n], rows[n + 1]) for n in range(0, len(rows), 2)]
+                to[slot, q : q + 8, :] = rows[0]
+
+    def integrate(t, slot):
+        piece = dot(left[slot].T, right[slot])
+        block_row = lax.rem(tiles_ref[0, t], block_rows)
+        block_col = tiles_ref[1, t]
         dest = lax.div(block_col, block_cols)
-        slot = count[dest]
-        count[dest] = slot + 1
-        label[2 * dest + slot] = block_row * block_cols + lax.rem(block_col, block_cols)
-        out_ref[dest, pl.ds(pl.multiple_of(slot * tile, tile), tile), :] = piece
-        return carry
-
-    lax.fori_loop(0, owned, one_tile, 0)
-    sublane = lax.broadcasted_iota(jnp.int32, (8, tile), 0)
+        place = count[dest]
+        count[dest] = place + 1
+        label[2 * dest + place] = block_row * block_cols + lax.rem(block_col, block_cols)
+        out_ref[dest, pl.ds(pl.multiple_of(place * tile, tile), tile), :] = piece
+
+    def two_tiles(n, carry):
+        gather(2 * n + 1, 1)
+        integrate(2 * n, 0)
+        gather(2 * n + 2, 0)
+        integrate(2 * n + 1, 1)
+        return carry
+
+    gather(0, 0)
+    lax.fori_loop(0, owned // 2 - 1, two_tiles, 0)
+    gather(owned - 1, 1)
+    integrate(owned - 2, 0)
+    integrate(owned - 1, 1)
     for d in range(dests):
         both = jnp.where(sublane == 0, label[2 * d], label[2 * d + 1])
         out_ref[d, 2 * tile : 2 * tile + 8, :] = both.astype(F32)
@@ -94,25 +123,26 @@
 def make_pieces(tile_list, tile_nodes, test_table, trial_table, dests):
     tile = test_table.shape[1]
     quad = tile_nodes.shape[1]
+    operands = (tile_list.T, tile_nodes, test_table, trial_table)
     return pl.pallas_call(
         pieces_kernel,
         out_shape=VMEM((dests, 2 * tile + 8, tile), F32),
-        in_specs=[
-            pl.BlockSpec(memory_space=pltpu.SMEM),
-            pl.BlockSpec(memory_space=pltpu.SMEM),
-            pl.BlockSpec(memory_space=VMEM),
-            pl.BlockSpec(memory_space=VMEM),
-        ],
+        in_specs=[pl.BlockSpec(memory_space=pltpu.HBM)] * 4,
         out_specs=pl.BlockSpec(memory_space=VMEM),
         scratch_shapes=[
-            VMEM((quad, tile), F32),
-            VMEM((quad, tile), F32),
+            VMEM(test_table.shape, F32),
+            VMEM(trial_table.shape, F32),
+            VMEM((2, quad, tile), F32),
+            VMEM((2, quad, tile), F32),
+            pltpu.SMEM(operands[0].shape, jnp.int32),
+            pltpu.SMEM(tile_nodes.shape, jnp.int32),
             pltpu.SMEM((dests,), jnp.int32),
             pltpu.SMEM((2 * dests,), jnp.int32),
+            DMA((4,)),
         ],
         compiler_params=pltpu.CompilerParams(vmem_limit_bytes=8 << 20),
         name="pieces",
-    )(tile_list, tile_nodes, test_table, trial_table)
+    )(*(pltpu.with_memory_space_constraint(operand, pltpu.HBM) for operand in operands))
 
 
 OFFSETS = sorted(
@@ -126,7 +156,7 @@
     return pltpu.with_memory_space_constraint(array, VMEM)
 
 
-def exchange_kernel(packed, far_hbm, s_hbm, arrived, far, g, strokes, send_sem, recv_sem, own_sem, far_sem, s_sem):
+def exchange_kernel(packed, far_hbm, s_hbm, arrived, far, strokes, send_sem, recv_sem, own_sem, far_sem, s_sem):
     row = lax.axis_index("row")
     col = lax.axis_index("col")
     x, y = lax.div(col, 4), lax.rem(col, 4)
@@ -159,11 +189,8 @@
     own = pltpu.make_async_copy(packed.at[col], arrived.at[col], own_sem)
     own.start()
     load_s.wait()
-    both = split(strokes[...])
-    for j in range(FAR_PARTS):
-        loads[j].wait()
-        part = pl.ds(j * size, size)
-        g[part, :] = dot_split(split(far[part, :]), both)
+    for load in loads:
+        load.wait()
     own.wait()
     for copy in copies:
         copy.wait()
@@ -178,11 +205,10 @@
         out_shape=(
             VMEM(packed.shape, F32),
             VMEM(far.shape, F32),
-            VMEM((far.shape[0], strokes.shape[1]), F32),
             VMEM(strokes.shape, F32),
         ),
         in_specs=[vmem, hbm, hbm],
-        out_specs=(vmem,) * 4,
+        out_specs=(vmem,) * 3,
         scratch_shapes=[DMA((n,)), DMA((n,)), DMA, DMA((FAR_PARTS,)), DMA],
         compiler_params=pltpu.CompilerParams(
             collective_id=0, has_side_effects=True, vmem_limit_bytes=8 << 20
@@ -195,7 +221,7 @@
     )
 
 
-def place_kernel(arrived, far, g0, strokes, out, g, label):
+def place_kernel(arrived, far, out, label):
     tile = arrived.shape[2]
     for d in range(arrived.shape[0]):
         for k in range(2):
@@ -211,37 +237,38 @@
             cols = pl.ds(pl.multiple_of(lax.rem(lab, 8) * tile, tile), tile)
             piece = arrived[lax.div(s, 2), pl.ds(pl.multiple_of(lax.rem(s, 2) * tile, tile), tile), :]
             out[rows, cols] = out[rows, cols] + piece
-            g[rows, :] = g[rows, :] + dot(piece, strokes[cols, :])
 
         return carry
 
     lax.fori_loop(0, label.shape[0], add, 0)
 
 
-def place(arrived, far, g, strokes):
+def place(arrived, far):
     vmem = pl.BlockSpec(memory_space=VMEM)
     return pl.pallas_call(
         place_kernel,
-        out_shape=(VMEM(far.shape, F32), VMEM(g.shape, F32)),
-        in_specs=[vmem] * 4,
-        out_specs=(vmem, vmem),
+        out_shape=VMEM(far.shape, F32),
+        in_specs=[vmem] * 2,
+        out_specs=vmem,
         scratch_shapes=[pltpu.SMEM((2 * arrived.shape[0],), jnp.int32)],
-        input_output_aliases={1: 0, 2: 1},
+        input_output_aliases={1: 0},
         compiler_params=pltpu.CompilerParams(vmem_limit_bytes=8 << 20),
         name="place",
-    )(resident(arrived), resident(far), resident(g), resident(strokes))
-
-
-P_CHUNKS = 32
-P_ROWS = 64
+    )(resident(arrived), resident(far))
+
+
+P_CHUNKS = 16
+P_ROWS = 128
 Q_CHUNKS = 16
 Q_ROWS = 32
-C_CHUNKS = 8
-LAG = 8
+C_CHUNKS = 4
+LAG = 4
+C_LAG = 2
+G_STEP = 1
 
 
 def panel_kernel(
-    asm, g_ref, inv_ref, s_ref, out_ref, img, p_ref, q_ref, c_ref, l_ref, u_ref, u_high, u_low, us_ref,
+    asm, inv_ref, s_ref, out_ref, img, g_ref, p_ref, q_ref, c_ref, l_ref, u_ref, u_high, u_low, us_ref,
     part, stage1, stage2, load_p, load_q, send_p, recv_p, send_q, recv_q, send_c, recv_c, send_i, recv_i
 ):
     row = lax.axis_index("row")
@@ -329,7 +356,9 @@
     lead = core == 0
     q_depth = [z + core, mod4(4 - z) + core]
     q_next = [(z_up, lead & (z < 3)), (z_down, lead & (z != 1))]
-    c_depth = 1 + LAG * (5 + jnp.where(z == 2, 2, jnp.where(z == 0, 0, 1)) + core)
+    deepest = jnp.maximum(jnp.maximum(depth[0], depth[1]), jnp.maximum(depth[2], depth[3]))
+    c_depth = 1 + LAG * deepest + C_LAG * (jnp.where(z == 2, 2, jnp.where(z == 0, 0, 1)) + core)
+    big = out_ref.shape[0] // 8
 
     def step(s, carry):
         for t in range(4):
@@ -392,9 +421,16 @@
                 def _():
                     c_copy(i, 1, z_up, False).start()
 
-        return carry
-
-    lax.fori_loop(0, max(P_CHUNKS + 5 * LAG, C_CHUNKS + 1 + 8 * LAG), step, 0)
+        n = s - G_STEP
+
+        @pl.when((n >= 0) & (n < 8))
+        def _():
+            mine = pl.ds(pl.multiple_of(n * big, big), big)
+            g_ref[mine, :] = dot(asm[mine, :], s_ref[...])
+
+        return carry
+
+    lax.fori_loop(0, max(P_CHUNKS + 5 * LAG, C_CHUNKS + 1 + 5 * LAG + 3 * C_LAG), step, 0)
 
     @pl.when(top)
     def _():
@@ -417,7 +453,6 @@
 
     rows = part.shape[0]
     half = rows // 2
-    big = half // 4
     small = big // 4
     outer = (x, y)
     inner = (y, x)
@@ -438,8 +473,8 @@
         )
 
     def first_copy(h, k):
-        to = mod4(jnp.where(h == 0, x, y) + k)
-        peer = jnp.where(h == 0, to * 4 + y, x * 4 + to)
+        to = mod4(outer[h] + k)
+        peer = to * 4 + y if h == 0 else x * 4 + to
         return remote(part.at[at(h * half + to * big, big), :], stage1.at[h, k - 1], 0, h, k, peer)
 
     def finish_tile(j, carry):
@@ -457,34 +492,39 @@
 
         return carry
 
-    def one_tile(n, carry):
-        h = lax.rem(n, 2)
-        k = table((2, 1, 3, 0), lax.div(n, 2))
-        j = h * 4 + mod4(jnp.where(h == 0, x, y) + k)
-        mine = at(j * big, big)
-        below0 = (row > 0) | (j > 0)
-        below1 = (row > 0) | (j > 1)
-        p0 = p_ref[mine, 0:256]
-        lower0 = jnp.where(below0, dot_split(split(p0), inv0), 0.0)
-        rest = p_ref[mine, 256:512] - dot(lower0, c_ref[0:256, :])
-        lower1 = jnp.where(below1, dot_split(split(rest), inv1), 0.0)
-        l_ref[mine, 0:256] = lower0
-        l_ref[mine, 256:512] = lower1
-        part[mine, :] = g_ref[mine, :] - dot(lower0, us_ref[0:256, :]) - dot(lower1, us_ref[256:512, :])
+    def two_tiles(n, carry):
+        k = table((2, 1, 3, 0), n)
+        tiles = []
+        for h in range(2):
+            j = h * 4 + mod4(outer[h] + k)
+            tiles.append((at(j * big, big), (row > 0) | (j > 0), (row > 0) | (j > 1)))
+        lower0 = [jnp.where(b0, dot_split(split(p_ref[m, 0:256]), inv0), 0.0) for m, b0, _ in tiles]
+        beside = split(c_ref[0:256, :])
+        rest = [p_ref[m, 256:512] - dot_split(split(low), beside) for (m, _, _), low in zip(tiles, lower0)]
+        lower1 = [jnp.where(b1, dot_split(split(r), inv1), 0.0) for (_, _, b1), r in zip(tiles, rest)]
+        us0, us1 = split(us_ref[0:256, :]), split(us_ref[256:512, :])
+        for (m, _, _), low0, low1 in zip(tiles, lower0, lower1):
+            l_ref[m, 0:256] = low0
+            l_ref[m, 256:512] = low1
+            part[m, :] = g_ref[m, :] - (dot_split(split(low0), us0) + dot_split(split(low1), us1))
 
         @pl.when(source)
         def _():
-            change0 = jnp.where(below0, lower0 - p0, 0.0)
-            change1 = jnp.where(below1, lower1 - rest, 0.0)
-            part[mine, :] += dot(change0, s_ref[0:256, :]) + dot(change1, s_ref[256:512, :])
+            for m, b0, b1 in tiles:
+                low0, low1 = l_ref[m, 0:256], l_ref[m, 256:512]
+                left = p_ref[m, 256:512] - dot(low0, c_ref[0:256, :])
+                change0 = jnp.where(b0, low0 - p_ref[m, 0:256], 0.0)
+                change1 = jnp.where(b1, low1 - left, 0.0)
+                part[m, :] += dot(change0, s_ref[0:256, :]) + dot(change1, s_ref[256:512, :])
 
         @pl.when(k > 0)
         def _():
-            first_copy(h, k).start()
-
-        return carry
-
-    lax.fori_loop(0, 8, one_tile, 0)
+            for h in range(2):
+                first_copy(h, k).start()
+
+        return carry
+
+    lax.fori_loop(0, 4, two_tiles, 0)
 
     order = (2, 1, 3)
     second, third, fourth = [], [], []
@@ -578,16 +618,17 @@
     lax.fori_loop(0, C_CHUNKS, drain_c, 0)
 
 
-def panels(asm, g, inverses, strokes):
+def panels(asm, inverses, strokes):
     rows, cols = asm.shape
     modes = strokes.shape[1]
     vmem = pl.BlockSpec(memory_space=VMEM)
     return pl.pallas_call(
         panel_kernel,
         out_shape=(VMEM((rows, cols), F32), VMEM((rows, modes), F32)),
-        in_specs=[vmem] * 4,
+        in_specs=[vmem] * 3,
         out_specs=(vmem, vmem),
         scratch_shapes=[
+            VMEM((rows, modes), F32),
             VMEM((rows, 512), F32),
             VMEM((512, cols), F32),
             VMEM((512, 256), F32),
@@ -614,14 +655,41 @@
             collective_id=1, has_side_effects=True, vmem_limit_bytes=32 << 20
         ),
         name="panels",
-    )(resident(asm), resident(g), inverses, resident(strokes))
+    )(resident(asm), inverses, resident(strokes))
+
+
+def hand_out_kernel(factored, image, factored_out, image_out, sem):
+    rows = factored.shape[0] // 4
+    copies = [
+        pltpu.make_async_copy(src.at[pl.ds(n * rows, rows)], dst.at[pl.ds(n * rows, rows)], sem.at[which, n])
+        for which, (src, dst) in enumerate(((factored, factored_out), (image, image_out)))
+        for n in range(4)
+    ]
+    for copy in copies:
+        copy.start()
+    for copy in copies:
+        copy.wait()
+
+
+def hand_out(factored, image):
+    vmem = pl.BlockSpec(memory_space=VMEM)
+    hbm = pl.BlockSpec(memory_space=pltpu.HBM)
+    return pl.pallas_call(
+        hand_out_kernel,
+        out_shape=(pltpu.HBM(factored.shape, F32), pltpu.HBM(image.shape, F32)),
+        in_specs=[vmem] * 2,
+        out_specs=(hbm, hbm),
+        scratch_shapes=[DMA((2, 4))],
+        compiler_params=pltpu.CompilerParams(vmem_limit_bytes=8 << 20),
+        name="hand_out",
+    )(resident(factored), resident(image))
 
 
 def on_device(far_field, inverses, test_table, trial_table, tile_list, tile_nodes, strokes):
     packed = make_pieces(tile_list, tile_nodes, test_table, trial_table, 16)
-    arrived, far, g, held_strokes = exchange(packed, far_field, strokes)
-    asm, g = place(arrived, far, g, held_strokes)
-    return panels(asm, g, inverses, held_strokes)
+    arrived, far, held_strokes = exchange(packed, far_field, strokes)
+    asm = place(arrived, far)
+    return hand_out(*panels(asm, inverses, held_strokes))
 
 
 def solution(mesh):

time: 149 us -> 138 us (0.926)
  local copies, waits for them, and re-layouts: 9.38 us -> 0.25 us
  Pallas kernels: 138 us -> 135 us
    unnamed x11 -> x2, local copies, waits for them, and re-layouts: 9.38 us -> 0.25 us
    pallas_call x1, Pallas kernels: 89.8 us -> 85 us  [panels(): pl.pallas_call(panel_kernel, out_shape=(VMEM((rows, cols), F32), VMEM((ro...]
    pallas_call x1 -> x2, Pallas kernels: 2.89 us -> 4.75 us  [the longest x1 3.98 us: hand_out(): pl.pallas_call(hand_out_kernel, out_shape=(pltpu.HBM(factored.shape, F32)...]
where the time goes in v4:
time: 138 us; the launch traced here: 136 us
  Pallas kernels  135 us (98%)
    pallas_call x1, Pallas kernels, panels(): pl.pallas_call(panel_kernel, out_shape=(VMEM((rows, cols), F32), VMEM((ro...  85 us
    pallas_call x1, Pallas kernels, exchange(): pl.pallas_call(exchange_kernel, out_shape=(VMEM(packed.shape, F32), VMEM(...  32.3 us
    pallas_call x1, Pallas kernels, make_pieces(): pl.pallas_call(pieces_kernel, out_shape=VMEM((dests, 2 * tile + 8, tile),...  12.7 us
    pallas_call x1, Pallas kernels, hand_out(): pl.pallas_call(hand_out_kernel, out_shape=(pltpu.HBM(factored.shape, F32)...  3.98 us

profile of v4, /device:TPU:72, one launch (start us, length us, event | category | flops | bytes accessed | tf_op | source)
XLA Modules:
  0.0 135.6 jit_solution(13727399904576924897)
XLA Ops:
  0.6 12.7 %pieces.1.packed = f32[16,264,128]{2,1,0:T(8,128)S(1)} custom-call(s32[2,16]{1,0:T(2,128)} %bitcast.1, s32[16,256]{1,0:T(8,128)} %nodes_hbm.1, f32[4096,128]{1,0:T(8,128)} %test_hbm.1, f32[4096,128]{1,0:T(8,128)} %trial_hbm.1), custom_call_target="tpu_custom_call" | custom-call | tf_op jit(solution)/shard_map/pieces/pallas_call | solution.py:127
  13.3 32.3 %exchange.1 = (f32[16,264,128]{2,1,0:T(8,128)S(1)}, f32[2048,1024]{1,0:T(8,128)S(1)}, f32[1024,256]{1,0:T(8,128)S(1)}) custom-call(f32[16,264,128]{2,1,0:T(8,128)S(1)} %pieces.1.packed, f32[2048,1024]{1,0:T(8,128)} %far_hbm.1, f32[1024,256]{1,0:T(8,128)} %s_hbm.1), custom_call_target="tpu_custom_call" | custom-call | tf_op jit(solution)/shard_map/exchange/pallas_call | solution.py:203
  45.6 0.0 copy-start
  45.6 0.8 place.1.asm
  46.4 0.2 copy-done
  46.6 85.0 %panels.1 = (f32[2048,1024]{1,0:T(8,128)S(1)}, f32[2048,256]{1,0:T(8,128)S(1)}) custom-call(f32[2048,1024]{1,0:T(8,128)S(1)} %place.1.asm, f32[2,256,256]{2,1,0:T(8,128)S(1)} %copy-done, f32[1024,256]{1,0:T(8,128)S(1)} %get-tuple-element.9.s_ref), custom_call_target="tpu_custom_call" | custom-call | tf_op jit(solution)/shard_map/panels/pallas_call | solution.py:625
  131.6 4.0 %hand_out.1 = (f32[2048,1024]{1,0:T(8,128)}, f32[2048,256]{1,0:T(8,128)}) custom-call(f32[2048,1024]{1,0:T(8,128)S(1)} %get-tuple-element.10.factored, f32[2048,256]{1,0:T(8,128)S(1)} %get-tuple-element.11.image), custom_call_target="tpu_custom_call" | custom-call | tf_op jit(solution)/shard_map/hand_out/pallas_call | solution.py:677
Async XLA Ops:
  45.6 1.0 copy-start

commit v5 on v4

--- a/solution.py
+++ b/solution.py
@@ -269,7 +269,8 @@
 
 def panel_kernel(
     asm, inv_ref, s_ref, out_ref, img, g_ref, p_ref, q_ref, c_ref, l_ref, u_ref, u_high, u_low, us_ref,
-    part, stage1, stage2, load_p, load_q, send_p, recv_p, send_q, recv_q, send_c, recv_c, send_i, recv_i
+    part, stage1, stage2, load_p, load_q, send_p, recv_p, send_q, recv_q, send_c, recv_c, send1, recv1, send2, recv2,
+    send3, recv3, send4, recv4
 ):
     row = lax.axis_index("row")
     col = lax.axis_index("col")
@@ -462,20 +463,30 @@
     def at(start, count):
         return pl.ds(pl.multiple_of(start, count), count)
 
-    def remote(src, dst, stage, h, k, peer):
+    def remote(src, dst, send, recv, peer):
         return pltpu.make_async_remote_copy(
-            src_ref=src,
-            dst_ref=dst,
-            send_sem=send_i.at[stage, h, k - 1],
-            recv_sem=recv_i.at[stage, h, k - 1],
-            device_id=(row, peer),
-            device_id_type=MESH,
+            src_ref=src, dst_ref=dst, send_sem=send, recv_sem=recv, device_id=(row, peer), device_id_type=MESH
         )
 
-    def first_copy(h, k):
-        to = mod4(outer[h] + k)
-        peer = to * 4 + y if h == 0 else x * 4 + to
-        return remote(part.at[at(h * half + to * big, big), :], stage1.at[h, k - 1], 0, h, k, peer)
+    def piece(h, m):
+        return at(mod4(inner[h] + m) * small, small)
+
+    def second_copy(h, m):
+        return remote(
+            stage1.at[h, 3, piece(h, m), :],
+            stage2.at[h, m - 1],
+            send2.at[h, m - 1],
+            recv2.at[h, m - 1],
+            inner_peers[h][m],
+        )
+
+    def third_copy(h, m):
+        here = img.at[at(h * half + outer[h] * big + inner[h] * small, small), :]
+        return remote(here, here, send3.at[h, m - 1], recv3.at[h, m - 1], inner_peers[h][m])
+
+    def fourth_copy(h, k, m):
+        here = img.at[at(h * half + outer[h] * big + mod4(inner[h] + 4 - m) * small, small), :]
+        return remote(here, here, send4.at[h, k - 1, m], recv4.at[h, k - 1, m], outer_peers[h][k])
 
     def finish_tile(j, carry):
         mine = at(j * big, big)
@@ -491,6 +502,19 @@
             out_ref[mine, 256:512] = l_ref[mine, 256:512]
 
         return carry
+
+    order = (2, 1, 3)
+    pieces = (2, 1, 3, 0)
+
+    def first_copy(h, k, m):
+        to = mod4(outer[h] + k)
+        return remote(
+            part.at[at(h * half + to * big + mod4(inner[h] + m) * small, small), :],
+            stage1.at[h, k - 1, piece(h, m), :],
+            send1.at[h, k - 1, m],
+            recv1.at[h, k - 1, m],
+            to * 4 + y if h == 0 else x * 4 + to,
+        )
 
     def two_tiles(n, carry):
         k = table((2, 1, 3, 0), n)
@@ -519,61 +543,55 @@
 
         @pl.when(k > 0)
         def _():
-            for h in range(2):
-                first_copy(h, k).start()
+            for m in pieces:
+                for h in range(2):
+                    first_copy(h, k, m).start()
 
         return carry
 
     lax.fori_loop(0, 4, two_tiles, 0)
 
-    order = (2, 1, 3)
-    second, third, fourth = [], [], []
+    for m in pieces:
+        for h in range(2):
+            for k in order:
+                first_copy(h, k, m).wait_recv()
+            total = part[at(h * half + outer[h] * big + mod4(inner[h] + m) * small, small), :]
+            for k in range(1, 4):
+                total = total + stage1[h, k - 1, piece(h, m), :]
+            stage1[h, 3, piece(h, m), :] = total
+            if m:
+                second_copy(h, m).start()
+    lax.fori_loop(0, 2, finish_tile, 0)
+    for h in range(2):
+        for m in order:
+            second_copy(h, m).wait_recv()
+        total = stage1[h, 3, piece(h, 0), :]
+        for m in range(1, 4):
+            total = total + stage2[h, m - 1]
+        img[at(h * half + outer[h] * big + inner[h] * small, small), :] = total
+        for m in order:
+            third_copy(h, m).start()
+        for k in order:
+            fourth_copy(h, k, 0).start()
+    lax.fori_loop(2, 4, finish_tile, 0)
+    for m in (1, 3, 2):
+        for h in range(2):
+            third_copy(h, m).wait_recv()
+            for k in order:
+                fourth_copy(h, k, m).start()
+    lax.fori_loop(4, 8, finish_tile, 0)
     for h in range(2):
         for k in order:
-            first_copy(h, k).wait_recv()
-        total = part[at(h * half + outer[h] * big, big), :]
-        for k in range(1, 4):
-            total = total + stage1[h, k - 1]
-        stage1[h, 3] = total
-        for k in order:
-            to = mod4(inner[h] + k)
-            copy = remote(
-                stage1.at[h, 3, at(to * small, small), :], stage2.at[h, k - 1], 1, h, k, inner_peers[h][k]
-            )
-            copy.start()
-            second.append((h, copy))
-    lax.fori_loop(0, 2, finish_tile, 0)
-    for h in range(2):
-        for g, copy in second:
-            if g == h:
-                copy.wait_recv()
-        total = stage1[h, 3, at(inner[h] * small, small), :]
-        for k in range(1, 4):
-            total = total + stage2[h, k - 1]
-        mine = at(h * half + outer[h] * big + inner[h] * small, small)
-        img[mine, :] = total
-        for k in order:
-            copy = remote(img.at[mine, :], img.at[mine, :], 2, h, k, inner_peers[h][k])
-            copy.start()
-            third.append((h, copy))
-    lax.fori_loop(2, 4, finish_tile, 0)
-    for h in range(2):
-        for g, copy in third:
-            if g == h:
-                copy.wait_recv()
-        mine = at(h * half + outer[h] * big, big)
-        for k in order:
-            copy = remote(img.at[mine, :], img.at[mine, :], 3, h, k, outer_peers[h][k])
-            copy.start()
-            fourth.append((h, copy))
-    lax.fori_loop(4, 8, finish_tile, 0)
-    for _, copy in fourth:
-        copy.wait_recv()
+            for m in range(4):
+                fourth_copy(h, k, m).wait_recv()
     for h in range(2):
         for k in order:
-            first_copy(h, k).wait_send()
-    for _, copy in second + third + fourth:
-        copy.wait_send()
+            second_copy(h, k).wait_send()
+            third_copy(h, k).wait_send()
+            for m in range(4):
+                first_copy(h, k, m).wait_send()
+                fourth_copy(h, k, m).wait_send()
+
     def drain_p(i, carry):
         for d in range(4):
 
@@ -648,8 +666,14 @@
             DMA((2, Q_CHUNKS)),
             DMA((C_CHUNKS, 3)),
             DMA((C_CHUNKS,)),
-            DMA((4, 2, 3)),
-            DMA((4, 2, 3)),
+            DMA((2, 3, 4)),
+            DMA((2, 3, 4)),
+            DMA((2, 3)),
+            DMA((2, 3)),
+            DMA((2, 3)),
+            DMA((2, 3)),
+            DMA((2, 3, 4)),
+            DMA((2, 3, 4)),
         ],
         compiler_params=pltpu.CompilerParams(
             collective_id=1, has_side_effects=True, vmem_limit_bytes=32 << 20

time: 138 us -> 136 us (0.986)
  no operation moved by 1% of the time
where the time goes in v5:
time: 136 us; the launch traced here: 135 us
  Pallas kernels  134 us (99%)
    pallas_call x1, Pallas kernels, panels(): pl.pallas_call(panel_kernel, out_shape=(VMEM((rows, cols), F32), VMEM((ro...  84.1 us
    pallas_call x1, Pallas kernels, exchange(): pl.pallas_call(exchange_kernel, out_shape=(VMEM(packed.shape, F32), VMEM(...  32.3 us
    pallas_call x1, Pallas kernels, make_pieces(): pl.pallas_call(pieces_kernel, out_shape=VMEM((dests, 2 * tile + 8, tile),...  12.7 us
    pallas_call x1, Pallas kernels, hand_out(): pl.pallas_call(hand_out_kernel, out_shape=(pltpu.HBM(factored.shape, F32)...  3.98 us

profile of v5, /device:TPU:72, one launch (start us, length us, event | category | flops | bytes accessed | tf_op | source)
XLA Modules:
  0.0 134.7 jit_solution(17909348927801028302)
XLA Ops:
  0.6 12.7 %pieces.1.packed = f32[16,264,128]{2,1,0:T(8,128)S(1)} custom-call(s32[2,16]{1,0:T(2,128)} %bitcast.1, s32[16,256]{1,0:T(8,128)} %nodes_hbm.1, f32[4096,128]{1,0:T(8,128)} %test_hbm.1, f32[4096,128]{1,0:T(8,128)} %trial_hbm.1), custom_call_target="tpu_custom_call" | custom-call | tf_op jit(solution)/shard_map/pieces/pallas_call | solution.py:127
  13.3 32.3 %exchange.1 = (f32[16,264,128]{2,1,0:T(8,128)S(1)}, f32[2048,1024]{1,0:T(8,128)S(1)}, f32[1024,256]{1,0:T(8,128)S(1)}) custom-call(f32[16,264,128]{2,1,0:T(8,128)S(1)} %pieces.1.packed, f32[2048,1024]{1,0:T(8,128)} %far_hbm.1, f32[1024,256]{1,0:T(8,128)} %s_hbm.1), custom_call_target="tpu_custom_call" | custom-call | tf_op jit(solution)/shard_map/exchange/pallas_call | solution.py:203
  45.6 0.0 copy-start
  45.6 0.8 place.1.asm
  46.4 0.2 copy-done
  46.6 84.1 %panels.1 = (f32[2048,1024]{1,0:T(8,128)S(1)}, f32[2048,256]{1,0:T(8,128)S(1)}) custom-call(f32[2048,1024]{1,0:T(8,128)S(1)} %place.1.asm, f32[2,256,256]{2,1,0:T(8,128)S(1)} %copy-done, f32[1024,256]{1,0:T(8,128)S(1)} %get-tuple-element.9.s_ref), custom_call_target="tpu_custom_call" | custom-call | tf_op jit(solution)/shard_map/panels/pallas_call | solution.py:643
  130.7 4.0 %hand_out.1 = (f32[2048,1024]{1,0:T(8,128)}, f32[2048,256]{1,0:T(8,128)}) custom-call(f32[2048,1024]{1,0:T(8,128)S(1)} %get-tuple-element.10.factored, f32[2048,256]{1,0:T(8,128)S(1)} %get-tuple-element.11.image), custom_call_target="tpu_custom_call" | custom-call | tf_op jit(solution)/shard_map/hand_out/pallas_call | solution.py:701
Async XLA Ops:
  45.6 1.0 copy-start

commit v6 on v5

--- a/solution.py
+++ b/solution.py
@@ -262,7 +262,7 @@
 Q_CHUNKS = 16
 Q_ROWS = 32
 C_CHUNKS = 4
-LAG = 4
+LAG = 3
 C_LAG = 2
 G_STEP = 1
 

time: 136 us -> 137 us (level)
  no operation moved by 1% of the time
where the time goes in v6:
time: 137 us; the launch traced here: 135 us
  Pallas kernels  134 us (98%)
    pallas_call x1, Pallas kernels, panels(): pl.pallas_call(panel_kernel, out_shape=(VMEM((rows, cols), F32), VMEM((ro...  84.3 us
    pallas_call x1, Pallas kernels, exchange(): pl.pallas_call(exchange_kernel, out_shape=(VMEM(packed.shape, F32), VMEM(...  32.3 us
    pallas_call x1, Pallas kernels, make_pieces(): pl.pallas_call(pieces_kernel, out_shape=VMEM((dests, 2 * tile + 8, tile),...  12.7 us
    pallas_call x1, Pallas kernels, hand_out(): pl.pallas_call(hand_out_kernel, out_shape=(pltpu.HBM(factored.shape, F32)...  3.98 us

profile of v6, /device:TPU:72, one launch (start us, length us, event | category | flops | bytes accessed | tf_op | source)
XLA Modules:
  0.0 134.9 jit_solution(10335992043409760156)
XLA Ops:
  0.6 12.7 %pieces.1.packed = f32[16,264,128]{2,1,0:T(8,128)S(1)} custom-call(s32[2,16]{1,0:T(2,128)} %bitcast.1, s32[16,256]{1,0:T(8,128)} %nodes_hbm.1, f32[4096,128]{1,0:T(8,128)} %test_hbm.1, f32[4096,128]{1,0:T(8,128)} %trial_hbm.1), custom_call_target="tpu_custom_call" | custom-call | tf_op jit(solution)/shard_map/pieces/pallas_call | solution.py:127
  13.3 32.3 %exchange.1 = (f32[16,264,128]{2,1,0:T(8,128)S(1)}, f32[2048,1024]{1,0:T(8,128)S(1)}, f32[1024,256]{1,0:T(8,128)S(1)}) custom-call(f32[16,264,128]{2,1,0:T(8,128)S(1)} %pieces.1.packed, f32[2048,1024]{1,0:T(8,128)} %far_hbm.1, f32[1024,256]{1,0:T(8,128)} %s_hbm.1), custom_call_target="tpu_custom_call" | custom-call | tf_op jit(solution)/shard_map/exchange/pallas_call | solution.py:203
  45.6 0.0 copy-start
  45.6 0.9 place.1.asm
  46.5 0.2 copy-done
  46.6 84.3 %panels.1 = (f32[2048,1024]{1,0:T(8,128)S(1)}, f32[2048,256]{1,0:T(8,128)S(1)}) custom-call(f32[2048,1024]{1,0:T(8,128)S(1)} %place.1.asm, f32[2,256,256]{2,1,0:T(8,128)S(1)} %copy-done, f32[1024,256]{1,0:T(8,128)S(1)} %get-tuple-element.9.s_ref), custom_call_target="tpu_custom_call" | custom-call | tf_op jit(solution)/shard_map/panels/pallas_call | solution.py:643
  131.0 4.0 %hand_out.1 = (f32[2048,1024]{1,0:T(8,128)}, f32[2048,256]{1,0:T(8,128)}) custom-call(f32[2048,1024]{1,0:T(8,128)S(1)} %get-tuple-element.10.factored, f32[2048,256]{1,0:T(8,128)S(1)} %get-tuple-element.11.image), custom_call_target="tpu_custom_call" | custom-call | tf_op jit(solution)/shard_map/hand_out/pallas_call | solution.py:701
Async XLA Ops:
  45.6 1.0 copy-start
